TPU v7x, 32 devices: a whole 2x2x4 slice. The times are simulated.
32 devices in a mesh: frag: 2 (over y), orb: 16 (over z, x, core).
Axes of the slice: x: 2, y: 2, z: 4, core: 2. Of those that a mesh axis runs over, the one named last changes fastest.
Arguments:
- slices: float32 [32, 640, 1024], P(('frag', 'orb')), parts along dimension 0, may hold values from -0.5 to 0.5
- occ_energy: float32 [32], P('frag'), parts along dimension 0, may hold values from -2 to -0.5
- virt_energy: float32 [1280], P('frag'), parts along dimension 0, may hold values from 0.3 to 3
- order: int32 [32], P('frag'), parts along dimension 0, may hold values from 0 to 15, each once
- near_keep: int32 [32], P(('frag', 'orb')), parts along dimension 0, may hold values 0 or 1
- far_keep: int32 [16], P('frag'), parts along dimension 0, may hold values 0 or 1
Outputs:
- density: float32 [32, 640, 1024], P(('frag', 'orb')), parts along dimension 0
There are 2 independent parts, one for each index of `frag`. A program takes and returns all parts, laid end to end along the dimension named above; each array names one. Nothing has to cross between parts.
Inputs may be any that keep to these rules, and one draw needn't show every extreme that they name: `order`: each position gets a different energy index.
All inputs are finite; a program needn't handle non-finite values. No bound on the sum of `near_keep` on one device may be relied on, other than what follows from the above.
Results may differ from a plain program's by a relative error of at most 0.0003.
Values sent between devices are 32-bit elements; how exact they have to be, the bound alone decides.
No kernel may reach another device: no remote copies, remote signals or barrier semaphores. Data moves between devices by JAX's collectives and lax.ppermute only.
A program may use at most 128 MiB of HBM per device.

v0:
```python
import jax
import jax.numpy as jnp
from jax import lax
from jax.experimental import pallas as pl
from jax.experimental.pallas import tpu as pltpu
from jax.sharding import PartitionSpec as P


NT = (((1,), (1,)), ((), ()))
NN = (((1,), (0,)), ((), ()))


def permute(block, pairs):
    return lax.ppermute(block, "orb", pairs)


def both_ways(pairs):
    return pairs + [(j, i) for i, j in pairs]


def split(x):
    high = x.astype(jnp.bfloat16)
    low = (x - high.astype(jnp.float32)).astype(jnp.bfloat16)
    return high, low


def put_left(ref, rows, x):
    high, low = split(x)
    k = x.shape[1]
    ref[rows, 0:k] = high
    ref[rows, k : 2 * k] = high
    ref[rows, 2 * k : 3 * k] = low


def put_right(ref, rows, x):
    high, low = split(x)
    k = x.shape[1]
    ref[rows, 0:k] = high
    ref[rows, k : 2 * k] = low
    ref[rows, 2 * k : 3 * k] = high


def dot(left, right, dims):
    return lax.dot_general(left, right, dims, preferred_element_type=jnp.float32)


def scalars(slot, order, occ, near, prev_near, far):
    n = lax.axis_size("orb")
    m = n // 2
    pos = lax.axis_index("orb")
    odd = lax.rem(pos, 2) == 1
    half = lax.rem(pos, m)
    special = (half == 0) | (half == m - 1)
    mate = jnp.where(odd, pos - 1, pos + 1)
    outer = lax.rem(jnp.where(odd, pos + 1, pos + n - 1), n)
    opposite = lax.rem(pos + m, n)
    if slot == "D":
        partner, weight = pos, jnp.float32(1.0)
    else:
        near_next = near[0].astype(jnp.float32)
        near_before = prev_near[0]
        mate_weight = jnp.where(odd, near_before, near_next)
        outer_weight = jnp.where(odd, near_next, near_before)
        far_weight = far[half].astype(jnp.float32)
        if slot == "A":
            partner, weight = mate, mate_weight
        else:
            ring = jnp.logical_not(special) if slot == "B" else special
            partner = jnp.where(ring, outer, opposite)
            weight = jnp.where(ring, outer_weight, far_weight)
    return occ[order[pos]] + occ[order[partner]], weight, special


def pair_kernel(slot, order, occ, near, prev_near, far, own, *rest):
    rest = list(rest)
    others = [own] if slot == "D" else [rest.pop(0) for _ in range(1 if slot == "A" else 2 if slot == "B" else 4)]
    vrow, vcol = rest.pop(0), rest.pop(0)
    acc = None if slot == "D" else rest.pop(0)
    out, left, right, wide, tall = rest
    total, weight, special = scalars(slot, order, occ, near, prev_near, far)
    put_left(left, slice(None), own[...])
    if slot in "DA":
        parts = [others[0][...]]
    elif slot == "B":
        parts = [jnp.where(special, others[1][...], others[0][...])]
    else:
        parts = [jnp.where(special, others[1][...], others[0][...]), jnp.where(special, others[3][...], others[2][...])]
    row = 0
    rows = own.shape[0]
    for part in parts:
        put_right(right, slice(row, row + part.shape[0]), part)
        row += part.shape[0]
    k = own.shape[1]
    coupling = dot(left[...], right[...], NT)
    amp = coupling / (total - vcol[...] - vrow[...])
    if slot == "D":
        tilde = amp
    else:
        tilde = (2.0 * amp - amp.T) * weight
    put_left(wide, slice(None), tilde)
    for i in range(3):
        tall[i * rows : (i + 1) * rows, :] = right[:, i * k : (i + 1) * k]
    result = dot(wide[...], tall[...], NN)
    if slot == "D":
        out[...] = result
    else:
        out[...] = acc[...] + result


def pair(slot, small, own, others, vrow, vcol, acc):
    rows, k = own.shape
    smem = pl.BlockSpec(memory_space=pltpu.SMEM)
    vmem = pl.BlockSpec(memory_space=pltpu.VMEM)
    operands = [*small, own, *others, vrow, vcol] + ([] if acc is None else [acc])
    in_specs = [smem] * len(small) + [vmem] * (len(operands) - len(small))
    return pl.pallas_call(
        lambda *refs: pair_kernel(slot, *refs),
        out_shape=jax.ShapeDtypeStruct((rows, k), jnp.float32),
        in_specs=in_specs,
        out_specs=vmem,
        scratch_shapes=[
            pltpu.VMEM((rows, 3 * k), jnp.bfloat16),
            pltpu.VMEM((rows, 3 * k), jnp.bfloat16),
            pltpu.VMEM((rows, 3 * rows), jnp.bfloat16),
            pltpu.VMEM((3 * rows, k), jnp.bfloat16),
        ],
        cost_estimate=pl.CostEstimate(
            flops=12 * rows * rows * k, bytes_accessed=12 * rows * k, transcendentals=0
        ),
    )(*operands)


def after(values, token):
    *values, token = lax.optimization_barrier((*values, token))
    return values, token


def body(slices, occ_energy, virt_energy, order, near_keep, far_keep):
    n = lax.axis_size("orb")
    m = n // 2
    specials = (0, m - 1, m, n - 1)
    mates = [(i, i ^ 1) for i in range(n)]
    outers = both_ways([(i, i + 1) for i in range(1, n - 1, 2) if i not in specials])
    straight = both_ways([(0, m), (m - 1, n - 1)])
    opposites = [(i, (i + m) % n) for i in range(n) if i not in specials]
    forwards = both_ways([(0, m - 1), (m, n - 1)])

    own = slices[0]
    rows = own.shape[0]
    cut = rows // 5 * 3
    pieces = (own[:cut], own[cut:])
    vrow = virt_energy[None, :]
    vcol = virt_energy[:, None]

    s0 = permute(pieces[0], straight)
    s1 = permute(pieces[1], straight)
    mate = permute(own, mates)
    prev_near = permute(near_keep.astype(jnp.float32), [(i, (i + 1) % n) for i in range(n)])
    outer = permute(own, outers)
    small = (order, occ_energy, near_keep, prev_near, far_keep)

    acc = pair("D", (order, occ_energy, near_keep, near_keep, far_keep), own, [], vrow, vcol, None)
    (s0w,), acc = after((s0,), acc)
    w0 = permute(s0w, forwards)
    acc = pair("A", small, own, [mate], vrow, vcol, acc)
    pieces, acc = after(pieces, acc)
    r0 = permute(pieces[0], opposites)
    r1 = permute(pieces[1], opposites)
    w1 = permute(s1, forwards)
    acc = pair("B", small, own, [outer, jnp.concatenate([s0, s1], axis=0)], vrow, vcol, acc)
    acc = pair("L", small, own, [r0, w0, r1, w1], vrow, vcol, acc)
    return acc[None]


def solution(mesh):
    return jax.shard_map(
        body,
        mesh=mesh,
        in_specs=(
            P(("frag", "orb"), None, None),
            P("frag"),
            P("frag"),
            P("frag"),
            P(("frag", "orb")),
            P("frag"),
        ),
        out_specs=P(("frag", "orb"), None, None),
        check_vma=False,
    )
```

profile of v0, /device:TPU:1, one launch (start us, length us, event | category | flops | bytes accessed | tf_op | source)
XLA Modules:
  0.0 175.3 jit_solution(17185363612757113901)
XLA Ops:
  0.0 0.0 collective-permute-start.1
  0.0 3.0 %slice_bitcast_fusion = f32[384,1024]{1,0:T(8,128)} fusion(f32[1,640,1024]{2,1,0:T(8,128)} %param.6), kind=kLoop, calls=%fused_computation.1 | loop fusion | bytes 3145728 | tf_op jit(solution)/shard_map/slice | solution.py:151
  3.0 1.8 %collective-permute-start.2 = (f32[384,1024]{1,0:T(8,128)}, f32[384,1024]{1,0:T(8,128)}, u32[]{:S(2)}, u32[]{:S(2)}) collective-permute-start(f32[384,1024]{1,0:T(8,128)} %slice_bitcast_fusion), channel_id=1, source_target_pairs={{0,8},{7,15},{8,0},{15,7},{16,24},{23,31},{24,16},{31,23}} | collective-permute-start | bytes 4718600 | tf_op jit(solution)/shard_map/ppermute | solution.py:14
  4.8 4.5 %collective-permute-start.8 = (f32[640,1024]{1,0:T(8,128)S(1)}, f32[640,1024]{1,0:T(8,128)}, u32[]{:S(2)}, u32[]{:S(2)}) collective-permute-start(f32[640,1024]{1,0:T(8,128)S(1)} %bitcast.11), channel_id=1, source_target_pairs={{1,2},{3,4},{5,6},{9,10},{11,12},{13,14},{2,1},{4,3},{6,5},{10,9},... | collective-permute-start | bytes 7864328 | tf_op jit(solution)/shard_map/ppermute | solution.py:14
  10.0 56.1 %collective-permute-start = (f32[1]{0:T(128)}, f32[1]{0:T(128)}, u32[]{:S(2)}, u32[]{:S(2)}) collective-permute-start(f32[1]{0:T(128)} %convert_element_type.3), channel_id=1, source_target_pairs={{0,1},{1,2},{2,3},{3,4},{4,5},{5,6},{6,7},{7,8},{8,9},{9,10},{10,1... | collective-permute-start | bytes 20 | tf_op jit(solution)/shard_map/ppermute | solution.py:14
  66.0 1.1 slice_bitcast_fusion.1
  67.1 1.7 collective-permute-start.6
  68.7 0.6 broadcast_in_dim.9.refs_6_.refs_7_.refs_8_.refs_10_
  69.3 0.9 broadcast_in_dim.12.refs_7_.refs_8_.refs_9_.refs_11_
  70.2 11.6 %shard_map.64.refs_9_ = f32[640,1024]{1,0:T(8,128)} custom-call(s32[16]{0:T(128)} %refs_0_.7, f32[16]{0:T(128)} %refs_1_.7, s32[1]{0:T(128)S(6)} %copy.11.refs_2_.refs_3_, s32[1]{0:T(128)S(6)} %copy.11.refs_2_.refs_3_, s32[8]{0:T(128)} %refs_4_.7, f32[640,1024]{1,0:T(8,128)} %bitcast.7, f32[1,640]{1,0:T(1,128)} %broadcast_in_dim.9.refs_6_.refs_7_.refs_8_.refs_10_, ...), custom_call_target="tpu_custom_call" | custom-call | flops 5033164800 | bytes 7864320 | tf_op jit(solution)/shard_map/pallas_call | solution.py:116
  81.8 0.0 collective-permute-done.2
  81.8 1.8 %collective-permute-start.4 = (f32[384,1024]{1,0:T(8,128)}, f32[384,1024]{1,0:T(8,128)}, u32[]{:S(2)}, u32[]{:S(2)}) collective-permute-start(f32[384,1024]{1,0:T(8,128)} %collective-permute-done.2), channel_id=1, source_target_pairs={{0,7},{8,15},{7,0},{15,8},{16,23},{24,31},{23,16},{31,24}} | collective-permute-start | bytes 4718600 | tf_op jit(solution)/shard_map/ppermute | solution.py:14
  83.6 0.0 collective-permute-done.1.refs_6_
  83.6 14.1 %shard_map.65.refs_10_ = f32[640,1024]{1,0:T(8,128)} custom-call(s32[16]{0:T(128)} %refs_0_.7, f32[16]{0:T(128)} %refs_1_.7, s32[1]{0:T(128)S(6)} %copy.11.refs_2_.refs_3_, f32[1]{0:T(128)} %collective-permute-done.refs_3_, s32[8]{0:T(128)} %refs_4_.7, f32[640,1024]{1,0:T(8,128)} %bitcast.8, f32[640,1024]{1,0:T(8,128)} %collective-permute-done.1.refs_6_, ...), custom_call_target="tpu_custom_call" | custom-call | flops 5033164800 | bytes 7864320 | tf_op jit(solution)/shard_map/pallas_call | solution.py:116
  97.7 4.2 %collective-permute-start.3 = (f32[384,1024]{1,0:T(8,128)}, f32[384,1024]{1,0:T(8,128)}, u32[]{:S(2)}, u32[]{:S(2)}) collective-permute-start(f32[384,1024]{1,0:T(8,128)} %slice_bitcast_fusion), channel_id=1, source_target_pairs={{1,9},{2,10},{3,11},{4,12},{5,13},{6,14},{9,1},{10,2},{11,3},{12,4... | collective-permute-start | bytes 4718600 | tf_op jit(solution)/shard_map/ppermute | solution.py:14
  102.0 0.0 collective-permute-done.6
  102.0 1.7 collective-permute-start.7
  103.6 2.1 %collective-permute-start.5 = (f32[256,1024]{1,0:T(8,128)}, f32[256,1024]{1,0:T(8,128)}, u32[]{:S(2)}, u32[]{:S(2)}) collective-permute-start(f32[256,1024]{1,0:T(8,128)} %slice_bitcast_fusion.1), channel_id=1, source_target_pairs={{1,9},{2,10},{3,11},{4,12},{5,13},{6,14},{9,1},{10,2},{11,3},{12,4... | collective-permute-start | bytes 3145736 | tf_op jit(solution)/shard_map/ppermute | solution.py:14
  105.8 3.6 %pad_maximum_fusion.refs_7_ = f32[640,1024]{1,0:T(8,128)} fusion(f32[256,1024]{1,0:T(8,128)} %collective-permute-done.6, f32[384,1024]{1,0:T(8,128)} %collective-permute-done.2), kind=kLoop, calls=%fused_computation | loop fusion | flops 655360 | bytes 5242880 | tf_op jit(solution)/shard_map/concatenate | solution.py:170
  109.3 0.0 collective-permute-done.8.refs_6_
  109.3 14.9 %shard_map.66.refs_12_ = f32[640,1024]{1,0:T(8,128)} custom-call(s32[16]{0:T(128)} %refs_0_.7, f32[16]{0:T(128)} %refs_1_.7, s32[1]{0:T(128)S(6)} %copy.11.refs_2_.refs_3_, f32[1]{0:T(128)} %collective-permute-done.refs_3_, s32[8]{0:T(128)} %refs_4_.7, f32[640,1024]{1,0:T(8,128)} %bitcast.9, f32[640,1024]{1,0:T(8,128)} %collective-permute-done.8.refs_6_, ...), custom_call_target="tpu_custom_call" | custom-call | flops 5033164800 | bytes 7864320 | tf_op jit(solution)/shard_map/pallas_call | solution.py:116
  124.2 36.2 %collective-permute-done.5.refs_8_ = f32[256,1024]{1,0:T(8,128)} collective-permute-done((f32[256,1024]{1,0:T(8,128)}, f32[256,1024]{1,0:T(8,128)}, u32[]{:S(2)}, u32[]{:S(2)}) %collective-permute-start.5) | collective-permute-done | bytes 1048608 | tf_op jit(solution)/shard_map/ppermute | solution.py:14
  160.4 0.0 collective-permute-done.3.refs_6_
  160.4 14.9 %shard_map.67 = f32[640,1024]{1,0:T(8,128)} custom-call(s32[16]{0:T(128)} %refs_0_.7, f32[16]{0:T(128)} %refs_1_.7, s32[1]{0:T(128)S(6)} %copy.11.refs_2_.refs_3_, f32[1]{0:T(128)} %collective-permute-done.refs_3_, s32[8]{0:T(128)} %refs_4_.7, f32[640,1024]{1,0:T(8,128)} %bitcast.10, f32[384,1024]{1,0:T(8,128)} %collective-permute-done.3.refs_6_, ...), custom_call_target="tpu_custom_call" | custom-call | flops 5033164800 | bytes 7864320 | tf_op jit(solution)/shard_map/pallas_call | solution.py:116
  (7 shorter events, 0.0 us)
Async XLA Ops:
  0.0 4.8 %copy-start = (f32[1,640,1024]{2,1,0:T(8,128)S(1)}, f32[1,640,1024]{2,1,0:T(8,128)}, u32[]{:S(2)}) copy-start(f32[1,640,1024]{2,1,0:T(8,128)} %param.6) | copy-start | bytes 7864324
  0.0 68.7 %copy-start.1 = (f32[640]{0:T(1024)S(1)}, f32[640]{0:T(1024)}, u32[]{:S(2)}) copy-start(f32[640]{0:T(1024)} %param.8) | copy-start | bytes 7684
  0.0 83.6 %collective-permute-start.1 = (f32[640,1024]{1,0:T(8,128)}, f32[640,1024]{1,0:T(8,128)}, u32[]{:S(2)}, u32[]{:S(2)}) collective-permute-start(f32[640,1024]{1,0:T(8,128)} %bitcast.6), channel_id=1, source_target_pairs={{0,1},{1,0},{2,3},{3,2},{4,5},{5,4},{6,7},{7,6},{8,9},{9,8},{10,11... | collective-permute-start | bytes 7864328 | tf_op jit(solution)/shard_map/ppermute | solution.py:14
  3.0 78.8 %collective-permute-start.2 = (f32[384,1024]{1,0:T(8,128)}, f32[384,1024]{1,0:T(8,128)}, u32[]{:S(2)}, u32[]{:S(2)}) collective-permute-start(f32[384,1024]{1,0:T(8,128)} %slice_bitcast_fusion), channel_id=1, source_target_pairs={{0,8},{7,15},{8,0},{15,7},{16,24},{23,31},{24,16},{31,23}} | collective-permute-start | bytes 4718600 | tf_op jit(solution)/shard_map/ppermute | solution.py:14
  4.8 104.5 %collective-permute-start.8 = (f32[640,1024]{1,0:T(8,128)S(1)}, f32[640,1024]{1,0:T(8,128)}, u32[]{:S(2)}, u32[]{:S(2)}) collective-permute-start(f32[640,1024]{1,0:T(8,128)S(1)} %bitcast.11), channel_id=1, source_target_pairs={{1,2},{3,4},{5,6},{9,10},{11,12},{13,14},{2,1},{4,3},{6,5},{10,9},... | collective-permute-start | bytes 7864328 | tf_op jit(solution)/shard_map/ppermute | solution.py:14
  10.0 73.7 %collective-permute-start = (f32[1]{0:T(128)}, f32[1]{0:T(128)}, u32[]{:S(2)}, u32[]{:S(2)}) collective-permute-start(f32[1]{0:T(128)} %convert_element_type.3), channel_id=1, source_target_pairs={{0,1},{1,2},{2,3},{3,4},{4,5},{5,6},{6,7},{7,8},{8,9},{9,10},{10,1... | collective-permute-start | bytes 20 | tf_op jit(solution)/shard_map/ppermute | solution.py:14
  67.1 34.9 %collective-permute-start.6 = (f32[256,1024]{1,0:T(8,128)}, f32[256,1024]{1,0:T(8,128)}, u32[]{:S(2)}, u32[]{:S(2)}) collective-permute-start(f32[256,1024]{1,0:T(8,128)} %slice_bitcast_fusion.1), channel_id=1, source_target_pairs={{0,8},{7,15},{8,0},{15,7},{16,24},{23,31},{24,16},{31,23}} | collective-permute-start | bytes 3145736 | tf_op jit(solution)/shard_map/ppermute | solution.py:14
  81.8 42.4 %collective-permute-start.4 = (f32[384,1024]{1,0:T(8,128)}, f32[384,1024]{1,0:T(8,128)}, u32[]{:S(2)}, u32[]{:S(2)}) collective-permute-start(f32[384,1024]{1,0:T(8,128)} %collective-permute-done.2), channel_id=1, source_target_pairs={{0,7},{8,15},{7,0},{15,8},{16,23},{24,31},{23,16},{31,24}} | collective-permute-start | bytes 4718600 | tf_op jit(solution)/shard_map/ppermute | solution.py:14
  97.7 62.7 %collective-permute-start.3 = (f32[384,1024]{1,0:T(8,128)}, f32[384,1024]{1,0:T(8,128)}, u32[]{:S(2)}, u32[]{:S(2)}) collective-permute-start(f32[384,1024]{1,0:T(8,128)} %slice_bitcast_fusion), channel_id=1, source_target_pairs={{1,9},{2,10},{3,11},{4,12},{5,13},{6,14},{9,1},{10,2},{11,3},{12,4... | collective-permute-start | bytes 4718600 | tf_op jit(solution)/shard_map/ppermute | solution.py:14
  102.0 22.3 %collective-permute-start.7 = (f32[256,1024]{1,0:T(8,128)}, f32[256,1024]{1,0:T(8,128)}, u32[]{:S(2)}, u32[]{:S(2)}) collective-permute-start(f32[256,1024]{1,0:T(8,128)} %collective-permute-done.6), channel_id=1, source_target_pairs={{0,7},{8,15},{7,0},{15,8},{16,23},{24,31},{23,16},{31,24}} | collective-permute-start | bytes 3145736 | tf_op jit(solution)/shard_map/ppermute | solution.py:14
  103.6 56.8 %collective-permute-start.5 = (f32[256,1024]{1,0:T(8,128)}, f32[256,1024]{1,0:T(8,128)}, u32[]{:S(2)}, u32[]{:S(2)}) collective-permute-start(f32[256,1024]{1,0:T(8,128)} %slice_bitcast_fusion.1), channel_id=1, source_target_pairs={{1,9},{2,10},{3,11},{4,12},{5,13},{6,14},{9,1},{10,2},{11,3},{12,4... | collective-permute-start | bytes 3145736 | tf_op jit(solution)/shard_map/ppermute | solution.py:14
where the time goes:
time: 176 us; the launch traced here: 175 us
  starting transfers between devices  73.8 us (42%)
  Pallas kernels  55.5 us (32%)
  waiting for transfers between devices  36.2 us (21%)
  local copies, waits for them, and re-layouts  5.54 us (3%)
  other arithmetic  3.55 us (2%)
    ppermute x9, starting transfers between devices, permute(): return lax.ppermute(block, 'orb', pairs)  73.8 us
    pallas_call x4, Pallas kernels, pair(): pl.pallas_call(lambda *refs: pair_kernel(slot, *refs), out_shape=jax.Shap...  55.5 us
    ppermute x9, waiting for transfers between devices, permute(): return lax.ppermute(block, 'orb', pairs)  36.2 us
    slice x2, local copies, waits for them, and re-layouts, body(): pieces = (own[:cut], own[cut:])  4.05 us
    concatenate x1, other arithmetic, body(): jnp.concatenate([s0, s1], axis=0)  3.55 us
  transfers between devices with their start and end apart: 9, of which 1 were waited for; matrix products, arithmetic and copies ran while one was open for 5% of the time, Pallas kernels for 23%

commit v1 on v0

v1 whole, which is shorter than its diff:
```python
import jax
import jax.numpy as jnp
from jax import lax
from jax.experimental import pallas as pl
from jax.experimental.pallas import tpu as pltpu
from jax.sharding import PartitionSpec as P


NT = (((1,), (1,)), ((), ()))
NN = (((1,), (0,)), ((), ()))


def permute(block, pairs):
    return lax.ppermute(block, "orb", pairs)


def both_ways(pairs):
    return pairs + [(j, i) for i, j in pairs]


def split(x):
    high = x.astype(jnp.bfloat16)
    low = (x - high.astype(jnp.float32)).astype(jnp.bfloat16)
    return high, low


def dot(left, right, dims):
    return lax.dot_general(left, right, dims, preferred_element_type=jnp.float32)


def put_wide(ref, x):
    high, low = split(x)
    k = x.shape[1]
    ref[:, 0:k] = high
    ref[:, k : 2 * k] = low
    ref[:, 2 * k : 3 * k] = high


def put_tall(ref, x):
    high, low = split(x)
    k = x.shape[0]
    ref[0:k] = high
    ref[k : 2 * k] = high
    ref[2 * k : 3 * k] = low


def product(wide, tall):
    return dot(wide[...], tall[...], NN)


def overlap(pair, tall):
    k = tall.shape[1]
    rows = tall.shape[0] // 3
    both = dot(pair[...], jnp.concatenate([tall[0:rows], tall[rows : 2 * rows]], axis=1), NT)
    return both + dot(pair[:, 0:k], tall[2 * rows : 3 * rows], NT)


def scalars(slot, order, occ, near, prev_near, far):
    n = lax.axis_size("orb")
    m = n // 2
    pos = lax.axis_index("orb")
    odd = lax.rem(pos, 2) == 1
    half = lax.rem(pos, m)
    special = (half == 0) | (half == m - 1)
    mate = jnp.where(odd, pos - 1, pos + 1)
    outer = lax.rem(jnp.where(odd, pos + 1, pos + n - 1), n)
    opposite = lax.rem(pos + m, n)
    if slot == "D":
        partner, weight = pos, jnp.float32(1.0)
    else:
        near_next = near[0].astype(jnp.float32)
        near_before = prev_near[0]
        mate_weight = jnp.where(odd, near_before, near_next)
        outer_weight = jnp.where(odd, near_next, near_before)
        far_weight = far[half].astype(jnp.float32)
        if slot == "A":
            partner, weight = mate, mate_weight
        else:
            ring = jnp.logical_not(special) if slot == "B" else special
            partner = jnp.where(ring, outer, opposite)
            weight = jnp.where(ring, outer_weight, far_weight)
    return occ[order[pos]] + occ[order[partner]], weight


def case(name):
    n = lax.axis_size("orb")
    m = n // 2
    half = lax.rem(lax.axis_index("orb"), m)
    special = (half == 0) | (half == m - 1)
    return special if name == "special" else jnp.logical_not(special)


def fetch(buffer, sem, sources):
    for name, source in sources:

        @pl.when(case(name))
        def _(source=source):
            copy = pltpu.make_async_copy(source, buffer, sem)
            copy.start()
            copy.wait()


def kernel_d(order, occ, own, vrow, vcol, out, own_pair, wide, tall):
    k = own.shape[1]
    high, low = split(own[...])
    own_pair[:, 0:k] = high
    own_pair[:, k : 2 * k] = low
    put_tall(tall, own[...])
    total, _ = scalars("D", order, occ, None, None, None)
    amp = overlap(own_pair, tall) / (total - vcol[...] - vrow[...])
    put_wide(wide, amp)
    out[...] = product(wide, tall)


def kernel_ab(slot, order, occ, near, prev_near, far, own_pair, *rest):
    *sources, vrow, vcol, acc, out, other, wide, tall, sem = rest
    if slot == "A":
        copy = pltpu.make_async_copy(sources[0], other, sem)
        copy.start()
        copy.wait()
    else:
        cut = sources[1].shape[0]
        fetch(other, sem, [("plain", sources[0])])
        fetch(other.at[0:cut], sem, [("special", sources[1])])
        fetch(other.at[cut:], sem, [("special", sources[2])])
    put_tall(tall, other[...])
    total, weight = scalars(slot, order, occ, near, prev_near, far)
    amp = overlap(own_pair, tall) / (total - vcol[...] - vrow[...])
    put_wide(wide, (2.0 * amp - amp.T) * weight)
    out[...] = acc[...] + product(wide, tall)


def kernel_l0(order, occ, near, prev_near, far, own_pair, late, rest, vrow, vcol, acc, out, amp_a, tall, other, wide, sem):
    cut = rest.shape[0]
    fetch(
        other,
        sem,
        [("special", late), ("plain", rest)],
    )
    put_tall(tall, other[...])
    total, weight = scalars("L", order, occ, near, prev_near, far)
    amp = overlap(own_pair, tall) / (total - vcol[...] - vrow[:, 0:cut])
    amp_a[...] = amp
    inner = amp[0:cut]
    put_wide(wide, (2.0 * inner - inner.T) * weight)
    out[0:cut] = acc[0:cut] + product(wide, tall)
    out[cut:] = acc[cut:]


def kernel_l1(
    order, occ, near, prev_near, far, own_pair, late, rest, vrow, vcol, acc, amp_a, tall_a,
    out, other, tall, wide_ab, wide_ba, wide_bb, sem,
):
    cut = amp_a.shape[1]
    fetch(
        other,
        sem,
        [("special", late), ("plain", rest)],
    )
    put_tall(tall, other[...])
    total, weight = scalars("L", order, occ, near, prev_near, far)
    amp = overlap(own_pair, tall) / (total - vcol[...] - vrow[:, cut:])
    across = amp_a[cut:]
    put_wide(wide_ab, (2.0 * amp[0:cut] - across.T) * weight)
    put_wide(wide_ba, (2.0 * across - amp[0:cut].T) * weight)
    put_wide(wide_bb, (2.0 * amp[cut:] - amp[cut:].T) * weight)
    out[0:cut] = acc[0:cut] + product(wide_ab, tall)
    out[cut:] = acc[cut:] + product(wide_ba, tall_a) + product(wide_bb, tall)


SMEM = pl.BlockSpec(memory_space=pltpu.SMEM)
VMEM = pl.BlockSpec(memory_space=pltpu.VMEM)
ANY = pl.BlockSpec(memory_space=pl.ANY)


def call(kernel, operands, outs, scratch, flops, limit=None):
    return pl.pallas_call(
        kernel,
        out_shape=[jax.ShapeDtypeStruct(shape, dtype) for shape, dtype in outs],
        in_specs=[spec for spec, _ in operands],
        out_specs=[VMEM] * len(outs),
        scratch_shapes=scratch,
        cost_estimate=pl.CostEstimate(flops=flops, bytes_accessed=8_000_000, transcendentals=0),
        compiler_params=pltpu.CompilerParams(vmem_limit_bytes=limit),
    )(*[value for _, value in operands])


def after(values, token):
    *values, token = lax.optimization_barrier((*values, token))
    return values, token


def body(slices, occ_energy, virt_energy, order, near_keep, far_keep):
    n = lax.axis_size("orb")
    m = n // 2
    specials = (0, m - 1, m, n - 1)
    mates = [(i, i ^ 1) for i in range(n)]
    outers = both_ways([(i, i + 1) for i in range(1, n - 1, 2) if i not in specials])
    straight = both_ways([(0, m), (m - 1, n - 1)])
    opposites = [(i, (i + m) % n) for i in range(n) if i not in specials]
    forwards = both_ways([(0, m - 1), (m, n - 1)])

    own = slices[0]
    rows, k = own.shape
    cut = rows // 5 * 3
    size = rows - cut
    bf16, f32 = jnp.bfloat16, jnp.float32
    pieces = (own[:cut], own[cut:])
    v = [(VMEM, virt_energy[None, :]), (VMEM, virt_energy[:, None])]
    flops = 12 * rows * rows * k

    prev_near = permute(near_keep.astype(f32), [(i, (i + 1) % n) for i in range(n)])
    straight_slices = [permute(pieces[0], straight), permute(pieces[1], straight)]
    mate = permute(own, mates)
    outer = permute(own, outers)
    small = [(SMEM, x) for x in (order, occ_energy, near_keep, prev_near, far_keep)]

    acc, own_pair = call(
        kernel_d, [small[0], small[1], (VMEM, own), *v],
        [((rows, k), f32), ((rows, 2 * k), bf16)],
        [pltpu.VMEM((rows, 3 * rows), bf16), pltpu.VMEM((3 * rows, k), bf16)],
        flops,
    )
    whole_scratch = [
        pltpu.VMEM((rows, k), f32),
        pltpu.VMEM((rows, 3 * rows), bf16),
        pltpu.VMEM((3 * rows, k), bf16),
        pltpu.SemaphoreType.DMA,
    ]
    (first, *pieces), acc = after((straight_slices[1], *pieces), acc)
    late1 = permute(first, forwards)
    rest = [permute(piece, opposites) for piece in pieces]
    late = [permute(straight_slices[0], forwards), late1]
    (acc,) = call(
        lambda *refs: kernel_ab("A", *refs),
        [*small, (VMEM, own_pair), (ANY, mate), *v, (VMEM, acc)],
        [((rows, k), f32)], whole_scratch, flops,
    )
    (acc,) = call(
        lambda *refs: kernel_ab("B", *refs),
        [*small, (VMEM, own_pair), (ANY, outer), (ANY, straight_slices[0]), (ANY, straight_slices[1]), *v, (VMEM, acc)],
        [((rows, k), f32)], whole_scratch, flops,
    )
    acc, amp_a, tall_a = call(
        kernel_l0,
        [*small, (VMEM, own_pair), (ANY, late[0]), (ANY, rest[0]), *v, (VMEM, acc)],
        [((rows, k), f32), ((rows, cut), f32), ((3 * cut, k), bf16)],
        [pltpu.VMEM((cut, k), f32), pltpu.VMEM((cut, 3 * cut), bf16), pltpu.SemaphoreType.DMA],
        flops // 2,
        26_000_000,
    )
    (acc,) = call(
        kernel_l1,
        [*small, (VMEM, own_pair), (ANY, late[1]), (ANY, rest[1]), *v, (VMEM, acc), (VMEM, amp_a), (VMEM, tall_a)],
        [((rows, k), f32)],
        [
            pltpu.VMEM((size, k), f32),
            pltpu.VMEM((3 * size, k), bf16),
            pltpu.VMEM((cut, 3 * size), bf16),
            pltpu.VMEM((size, 3 * cut), bf16),
            pltpu.VMEM((size, 3 * size), bf16),
            pltpu.SemaphoreType.DMA,
        ],
        flops // 2,
        26_000_000,
    )
    return acc[None]


def solution(mesh):
    return jax.shard_map(
        body,
        mesh=mesh,
        in_specs=(
            P(("frag", "orb"), None, None),
            P("frag"),
            P("frag"),
            P("frag"),
            P(("frag", "orb")),
            P("frag"),
        ),
        out_specs=P(("frag", "orb"), None, None),
        check_vma=False,
    )
```

time: 176 us -> 190 us (1.080)
  the two profiles are of different devices: /device:TPU:1 before, /device:TPU:0 now
where the time goes in v1:
time: 190 us
  waiting for transfers between devices  103 us (54%)
  Pallas kernels  58.3 us (31%)
  starting transfers between devices  19.5 us (10%)
  local copies, waits for them, and re-layouts  8.27 us (4%)
    ppermute x9, waiting for transfers between devices, permute(): return lax.ppermute(block, 'orb', pairs)  103 us
    pallas_call x5, Pallas kernels, call(): pl.pallas_call(kernel, out_shape=[jax.ShapeDtypeStruct(shape, dtype) for...  58.3 us
    ppermute x9, starting transfers between devices, permute(): return lax.ppermute(block, 'orb', pairs)  19.5 us
    slice x2, local copies, waits for them, and re-layouts, body(): pieces = (own[:cut], own[cut:])  5.02 us
  transfers between devices with their start and end apart: 9, of which 2 were waited for; matrix products, arithmetic and copies ran while one was open for 3% of the time, Pallas kernels for 26%

profile of v1, /device:TPU:0, one launch (start us, length us, event | category | flops | bytes accessed | tf_op | source)
XLA Modules:
  0.0 189.8 jit_solution(11267230275046693535)
XLA Ops:
  0.0 0.5 collective-permute-start.8
  0.5 2.7 %slice_bitcast_fusion = f32[384,1024]{1,0:T(8,128)} fusion(f32[1,640,1024]{2,1,0:T(8,128)} %param.6), kind=kLoop, calls=%fused_computation | loop fusion | bytes 3145728 | tf_op jit(solution)/shard_map/slice | solution.py:208
  3.2 5.5 %collective-permute-start.4 = (f32[384,1024]{1,0:T(8,128)}, f32[384,1024]{1,0:T(8,128)}, u32[]{:S(2)}, u32[]{:S(2)}) collective-permute-start(f32[384,1024]{1,0:T(8,128)} %slice_bitcast_fusion), channel_id=1, source_target_pairs={{0,8},{7,15},{8,0},{15,7},{16,24},{23,31},{24,16},{31,23}} | collective-permute-start | bytes 4718600 | tf_op jit(solution)/shard_map/ppermute | solution.py:14
  8.7 2.2 %collective-permute-start.7 = (f32[640,1024]{1,0:T(8,128)}, f32[640,1024]{1,0:T(8,128)}, u32[]{:S(2)}, u32[]{:S(2)}) collective-permute-start(f32[640,1024]{1,0:T(8,128)} %bitcast.own), channel_id=1, source_target_pairs={{1,2},{3,4},{5,6},{9,10},{11,12},{13,14},{2,1},{4,3},{6,5},{10,9},... | collective-permute-start | bytes 7864328 | tf_op jit(solution)/shard_map/ppermute | solution.py:14
  10.9 2.3 %slice_bitcast_fusion.1 = f32[256,1024]{1,0:T(8,128)} fusion(f32[1,640,1024]{2,1,0:T(8,128)} %param.6), kind=kLoop, calls=%fused_computation.1 | loop fusion | bytes 2097152 | tf_op jit(solution)/shard_map/slice | solution.py:208
  13.2 1.9 %collective-permute-start.1 = (f32[256,1024]{1,0:T(8,128)}, f32[256,1024]{1,0:T(8,128)}, u32[]{:S(2)}, u32[]{:S(2)}) collective-permute-start(f32[256,1024]{1,0:T(8,128)} %slice_bitcast_fusion.1), channel_id=1, source_target_pairs={{0,8},{7,15},{8,0},{15,7},{16,24},{23,31},{24,16},{31,23}} | collective-permute-start | bytes 3145736 | tf_op jit(solution)/shard_map/ppermute | solution.py:14
  15.1 0.9 broadcast_in_dim.12.vcol.refs_8_.refs_10_
  16.0 0.6 broadcast_in_dim.9.vrow.refs_7_.refs_9_
  16.6 11.6 %shard_map.64 = (f32[640,1024]{1,0:T(8,128)}, bf16[640,2048]{1,0:T(8,128)(2,1)}) custom-call(s32[16]{0:T(128)} %order.5, f32[16]{0:T(128)} %occ.5, f32[640,1024]{1,0:T(8,128)} %bitcast.own, f32[1,640]{1,0:T(1,128)} %broadcast_in_dim.9.vrow.refs_7_.refs_9_, f32[640,1]{1,0:T(8,128)} %broadcast_in_dim.12.vcol.refs_8_.refs_10_), custom_call_target="tpu_custom_call" | custom-call | flops 5033164800 | bytes 8000000 | tf_op jit(solution)/shard_map/pallas_call | solution.py:177
  28.2 73.0 %collective-permute-done.1.refs_8_ = f32[256,1024]{1,0:T(8,128)} collective-permute-done((f32[256,1024]{1,0:T(8,128)}, f32[256,1024]{1,0:T(8,128)}, u32[]{:S(2)}, u32[]{:S(2)}) %collective-permute-start.1) | collective-permute-done | bytes 1048608 | tf_op jit(solution)/shard_map/ppermute | solution.py:14
  101.2 1.8 collective-permute-start.6
  103.0 3.1 %collective-permute-start.5 = (f32[384,1024]{1,0:T(8,128)}, f32[384,1024]{1,0:T(8,128)}, u32[]{:S(2)}, u32[]{:S(2)}) collective-permute-start(f32[384,1024]{1,0:T(8,128)} %collective-permute-done.4.refs_7_), channel_id=1, source_target_pairs={{0,7},{8,15},{7,0},{15,8},{16,23},{24,31},{23,16},{31,24}} | collective-permute-start | bytes 4718600 | tf_op jit(solution)/shard_map/ppermute | solution.py:14
  106.7 0.9 collective-permute-start
  107.6 29.7 %collective-permute-done.refs_3_.prev_near = f32[1]{0:T(128)} collective-permute-done((f32[1]{0:T(128)}, f32[1]{0:T(128)}, u32[]{:S(2)}, u32[]{:S(2)}) %collective-permute-start) | collective-permute-done | bytes 36 | tf_op jit(solution)/shard_map/ppermute | solution.py:14
  137.2 1.9 %collective-permute-start.2 = (f32[256,1024]{1,0:T(8,128)}, f32[256,1024]{1,0:T(8,128)}, u32[]{:S(2)}, u32[]{:S(2)}) collective-permute-start(f32[256,1024]{1,0:T(8,128)} %collective-permute-done.1.refs_8_), channel_id=1, source_target_pairs={{0,7},{8,15},{7,0},{15,8},{16,23},{24,31},{23,16},{31,24}} | collective-permute-start | bytes 3145736 | tf_op jit(solution)/shard_map/ppermute | solution.py:14
  139.2 1.8 collective-permute-start.3
  141.0 15.2 %shard_map.65.refs_11_ = f32[640,1024]{1,0:T(8,128)} custom-call(s32[16]{0:T(128)} %order.5, f32[16]{0:T(128)} %occ.5, s32[1]{0:T(128)S(6)} %copy.12.refs_2_.near, f32[1]{0:T(128)} %collective-permute-done.refs_3_.prev_near, s32[8]{0:T(128)} %far.3, bf16[640,2048]{1,0:T(8,128)(2,1)} %get-tuple-element.14.refs_5_.own_pair, f32[640,1024]{1,0:T(8,128)} %copy-done.8, ...), custom_call_target="tpu_custom_call" | custom-call | flops 5033164800 | bytes 8000000 | tf_op jit(solution)/shard_map/pallas_call | solution.py:177
  156.2 0.0 copy-start.3
  156.2 0.0 copy-start.4
  156.2 0.0 copy-start.5
  156.3 16.2 %shard_map.66.acc = f32[640,1024]{1,0:T(8,128)} custom-call(s32[16]{0:T(128)} %order.5, f32[16]{0:T(128)} %occ.5, s32[1]{0:T(128)S(6)} %copy.12.refs_2_.near, f32[1]{0:T(128)} %collective-permute-done.refs_3_.prev_near, s32[8]{0:T(128)} %far.3, bf16[640,2048]{1,0:T(8,128)(2,1)} %get-tuple-element.14.refs_5_.own_pair, ...), custom_call_target="tpu_custom_call" | custom-call | flops 5033164800 | bytes 8000000 | tf_op jit(solution)/shard_map/pallas_call | solution.py:177
  172.6 1.7 copy-done.6
  174.3 6.3 %shard_map.67 = (f32[640,1024]{1,0:T(8,128)S(1)}, f32[640,384]{1,0:T(8,128)S(1)}, bf16[1152,1024]{1,0:T(8,128)(2,1)S(1)}) custom-call(s32[16]{0:T(128)S(1)} %copy-done.3, f32[16]{0:T(128)S(1)} %copy-done.4, s32[1]{0:T(128)S(6)} %copy.12.refs_2_.near, f32[1]{0:T(128)} %collective-permute-done.refs_3_.prev_near, s32[8]{0:T(128)S(1)} %copy-done.5, ...), custom_call_target="tpu_custom_call" | custom-call | flops 2516582400 | bytes 8000000 | tf_op jit(solution)/shard_map/pallas_call | solution.py:177
  180.7 8.9 %shard_map.68 = f32[640,1024]{1,0:T(8,128)} custom-call(s32[16]{0:T(128)S(1)} %copy-done.3, f32[16]{0:T(128)S(1)} %copy-done.4, s32[1]{0:T(128)S(6)} %copy.12.refs_2_.near, f32[1]{0:T(128)} %collective-permute-done.refs_3_.prev_near, s32[8]{0:T(128)S(1)} %copy-done.5, bf16[640,2048]{1,0:T(8,128)(2,1)S(1)} %copy-done, ...), custom_call_target="tpu_custom_call" | custom-call | flops 2516582400 | bytes 8000000 | tf_op jit(solution)/shard_map/pallas_call | solution.py:177
  (21 shorter events, 0.0 us)
Async XLA Ops:
  0.0 15.1 %copy-start.7 = (f32[640]{0:T(1024)S(1)}, f32[640]{0:T(1024)}, u32[]{:S(2)}) copy-start(f32[640]{0:T(1024)} %param.8) | copy-start | bytes 7684
  0.0 139.2 %collective-permute-start.8 = (f32[640,1024]{1,0:T(8,128)}, f32[640,1024]{1,0:T(8,128)S(1)}, u32[]{:S(2)}, u32[]{:S(2)}) collective-permute-start(f32[640,1024]{1,0:T(8,128)} %bitcast.own), channel_id=1, source_target_pairs={{0,1},{1,0},{2,3},{3,2},{4,5},{5,4},{6,7},{7,6},{8,9},{9,8},{10,11... | collective-permute-start | bytes 7864328 | tf_op jit(solution)/shard_map/ppermute | solution.py:14
  3.2 99.7 %collective-permute-start.4 = (f32[384,1024]{1,0:T(8,128)}, f32[384,1024]{1,0:T(8,128)}, u32[]{:S(2)}, u32[]{:S(2)}) collective-permute-start(f32[384,1024]{1,0:T(8,128)} %slice_bitcast_fusion), channel_id=1, source_target_pairs={{0,8},{7,15},{8,0},{15,7},{16,24},{23,31},{24,16},{31,23}} | collective-permute-start | bytes 4718600 | tf_op jit(solution)/shard_map/ppermute | solution.py:14
  8.7 147.6 %collective-permute-start.7 = (f32[640,1024]{1,0:T(8,128)}, f32[640,1024]{1,0:T(8,128)}, u32[]{:S(2)}, u32[]{:S(2)}) collective-permute-start(f32[640,1024]{1,0:T(8,128)} %bitcast.own), channel_id=1, source_target_pairs={{1,2},{3,4},{5,6},{9,10},{11,12},{13,14},{2,1},{4,3},{6,5},{10,9},... | collective-permute-start | bytes 7864328 | tf_op jit(solution)/shard_map/ppermute | solution.py:14
  13.2 88.0 %collective-permute-start.1 = (f32[256,1024]{1,0:T(8,128)}, f32[256,1024]{1,0:T(8,128)}, u32[]{:S(2)}, u32[]{:S(2)}) collective-permute-start(f32[256,1024]{1,0:T(8,128)} %slice_bitcast_fusion.1), channel_id=1, source_target_pairs={{0,8},{7,15},{8,0},{15,7},{16,24},{23,31},{24,16},{31,23}} | collective-permute-start | bytes 3145736 | tf_op jit(solution)/shard_map/ppermute | solution.py:14
  101.2 71.4 %collective-permute-start.6 = (f32[384,1024]{1,0:T(8,128)}, f32[384,1024]{1,0:T(8,128)}, u32[]{:S(2)}, u32[]{:S(2)}) collective-permute-start(f32[384,1024]{1,0:T(8,128)} %slice_bitcast_fusion), channel_id=1, source_target_pairs={{1,9},{2,10},{3,11},{4,12},{5,13},{6,14},{9,1},{10,2},{11,3},{12,4... | collective-permute-start | bytes 4718600 | tf_op jit(solution)/shard_map/ppermute | solution.py:14
  103.0 69.6 %collective-permute-start.5 = (f32[384,1024]{1,0:T(8,128)}, f32[384,1024]{1,0:T(8,128)}, u32[]{:S(2)}, u32[]{:S(2)}) collective-permute-start(f32[384,1024]{1,0:T(8,128)} %collective-permute-done.4.refs_7_), channel_id=1, source_target_pairs={{0,7},{8,15},{7,0},{15,8},{16,23},{24,31},{23,16},{31,24}} | collective-permute-start | bytes 4718600 | tf_op jit(solution)/shard_map/ppermute | solution.py:14
  106.7 30.5 %collective-permute-start = (f32[1]{0:T(128)}, f32[1]{0:T(128)}, u32[]{:S(2)}, u32[]{:S(2)}) collective-permute-start(f32[1]{0:T(128)} %convert_element_type.3), channel_id=1, source_target_pairs={{0,1},{1,2},{2,3},{3,4},{4,5},{5,6},{6,7},{7,8},{8,9},{9,10},{10,1... | collective-permute-start | bytes 20 | tf_op jit(solution)/shard_map/ppermute | solution.py:14
  137.2 43.4 %collective-permute-start.2 = (f32[256,1024]{1,0:T(8,128)}, f32[256,1024]{1,0:T(8,128)}, u32[]{:S(2)}, u32[]{:S(2)}) collective-permute-start(f32[256,1024]{1,0:T(8,128)} %collective-permute-done.1.refs_8_), channel_id=1, source_target_pairs={{0,7},{8,15},{7,0},{15,8},{16,23},{24,31},{23,16},{31,24}} | collective-permute-start | bytes 3145736 | tf_op jit(solution)/shard_map/ppermute | solution.py:14
  139.2 1.8 copy-start.8
  139.2 41.5 %collective-permute-start.3 = (f32[256,1024]{1,0:T(8,128)}, f32[256,1024]{1,0:T(8,128)}, u32[]{:S(2)}, u32[]{:S(2)}) collective-permute-start(f32[256,1024]{1,0:T(8,128)} %slice_bitcast_fusion.1), channel_id=1, source_target_pairs={{1,9},{2,10},{3,11},{4,12},{5,13},{6,14},{9,1},{10,2},{11,3},{12,4... | collective-permute-start | bytes 3145736 | tf_op jit(solution)/shard_map/ppermute | solution.py:14
  156.2 16.4 %copy-start = (bf16[640,2048]{1,0:T(8,128)(2,1)S(1)}, bf16[640,2048]{1,0:T(8,128)(2,1)}, u32[]{:S(2)}) copy-start(bf16[640,2048]{1,0:T(8,128)(2,1)} %get-tuple-element.14.refs_5_.own_pair) | copy-start | bytes 7864324
  156.2 16.4 %copy-start.1 = (f32[640,1]{1,0:T(8,128)S(1)}, f32[640,1]{1,0:T(8,128)}, u32[]{:S(2)}) copy-start(f32[640,1]{1,0:T(8,128)} %broadcast_in_dim.12.vcol.refs_8_.refs_10_) | copy-start | bytes 7684
  156.2 16.4 %copy-start.2 = (f32[1,640]{1,0:T(1,128)S(1)}, f32[1,640]{1,0:T(1,128)}, u32[]{:S(2)}) copy-start(f32[1,640]{1,0:T(1,128)} %broadcast_in_dim.9.vrow.refs_7_.refs_9_) | copy-start | bytes 7684
  156.2 16.4 %copy-start.3 = (s32[16]{0:T(128)S(1)}, s32[16]{0:T(128)}, u32[]{:S(2)}) copy-start(s32[16]{0:T(128)} %order.5) | copy-start | bytes 196
  156.2 16.3 %copy-start.4 = (f32[16]{0:T(128)S(1)}, f32[16]{0:T(128)}, u32[]{:S(2)}) copy-start(f32[16]{0:T(128)} %occ.5) | copy-start | bytes 196
  156.2 16.3 %copy-start.5 = (s32[8]{0:T(128)S(1)}, s32[8]{0:T(128)}, u32[]{:S(2)}) copy-start(s32[8]{0:T(128)} %far.3) | copy-start | bytes 100
  172.6 1.7 copy-start.6

commit v2 on v1

v2 whole, which is shorter than its diff:
```python
import jax
import jax.numpy as jnp
from jax import lax
from jax.experimental import pallas as pl
from jax.experimental.pallas import tpu as pltpu
from jax.sharding import PartitionSpec as P


NT = (((1,), (1,)), ((), ()))
NN = (((1,), (0,)), ((), ()))


def permute(block, pairs):
    return lax.ppermute(block, "orb", pairs)


def both_ways(pairs):
    return pairs + [(j, i) for i, j in pairs]


def split(x):
    high = x.astype(jnp.bfloat16)
    low = (x - high.astype(jnp.float32)).astype(jnp.bfloat16)
    return high, low


def dot(left, right, dims):
    return lax.dot_general(left, right, dims, preferred_element_type=jnp.float32)


def put_tall(ref, x):
    high, low = split(x)
    k = x.shape[0]
    ref[0:k] = high
    ref[k : 2 * k] = high
    ref[2 * k : 3 * k] = low


def put_wide(ref, x):
    high, low = split(x)
    k = x.shape[1]
    ref[:, 0:k] = high
    ref[:, k : 2 * k] = low
    ref[:, 2 * k : 3 * k] = high


def overlap(own, right):
    half = own.shape[0] // 2
    return jnp.concatenate(
        [dot(own[0:half], right[...], NT), dot(own[half:], right[...], NT)], axis=0
    )


def column_blocks(k):
    width = k // 4
    return [slice(i * width, (i + 1) * width) for i in range(4)]


def scalars(slot, order, occ, near, prev_near, far):
    n = lax.axis_size("orb")
    m = n // 2
    pos = lax.axis_index("orb")
    odd = lax.rem(pos, 2) == 1
    half = lax.rem(pos, m)
    special = (half == 0) | (half == m - 1)
    mate = jnp.where(odd, pos - 1, pos + 1)
    outer = lax.rem(jnp.where(odd, pos + 1, pos + n - 1), n)
    opposite = lax.rem(pos + m, n)
    if slot == "D":
        partner, weight = pos, jnp.float32(1.0)
    else:
        near_next = near[0].astype(jnp.float32)
        near_before = prev_near[0]
        mate_weight = jnp.where(odd, near_before, near_next)
        outer_weight = jnp.where(odd, near_next, near_before)
        far_weight = far[half].astype(jnp.float32)
        if slot == "A":
            partner, weight = mate, mate_weight
        else:
            ring = jnp.logical_not(special) if slot == "B" else special
            partner = jnp.where(ring, outer, opposite)
            weight = jnp.where(ring, outer_weight, far_weight)
    return occ[order[pos]] + occ[order[partner]], weight


def case(name):
    n = lax.axis_size("orb")
    m = n // 2
    half = lax.rem(lax.axis_index("orb"), m)
    special = (half == 0) | (half == m - 1)
    return special if name == "special" else jnp.logical_not(special)


def fetch(buffer, sem, sources):
    for name, source in sources:

        @pl.when(case(name))
        def _(source=source):
            copy = pltpu.make_async_copy(source, buffer, sem)
            copy.start()
            copy.wait()


def kernel_d(order, occ, own, vrow, vcol, out, own_three, right, wide, tall):
    k = own.shape[1]
    high, low = split(own[...])
    own_three[:, 0:k] = high
    own_three[:, k : 2 * k] = high
    own_three[:, 2 * k : 3 * k] = low
    put_wide(right, own[...])
    put_tall(tall, own[...])
    total, _ = scalars("D", order, occ, None, None, None)
    put_wide(wide, overlap(own_three, right) / (total - vcol[...] - vrow[...]))
    for columns in column_blocks(k):
        out[:, columns] = dot(wide[...], tall[:, columns], NN)


def kernel_ab(slot, *refs):
    if slot == "A":
        order, occ, near, prev_near, far, own, other, vrow, vcol, acc, out, later, right, wide, tall = refs
        total, weight = scalars("A", order, occ, near, prev_near, far)
        for i, name in enumerate("BL"):
            for j, value in enumerate(scalars(name, order, occ, near, prev_near, far)):
                later[2 * i + j : 2 * i + j + 1] = jnp.full((1, later.shape[1]), value, jnp.float32)
    else:
        later, own, plain, special0, special1, vrow, vcol, acc, out, other, right, wide, tall, sem = refs
        total, weight = later[0:1, 0:1], later[1:2, 0:1]
        cut = special0.shape[0]
        fetch(other, sem, [("plain", plain)])
        fetch(other.at[0:cut], sem, [("special", special0)])
        fetch(other.at[cut:], sem, [("special", special1)])
    put_wide(right, other[...])
    put_tall(tall, other[...])
    amp = overlap(own, right) / (total - vcol[...] - vrow[...])
    put_wide(wide, (2.0 * amp - amp.T) * weight)
    for columns in column_blocks(acc.shape[1]):
        out[:, columns] = acc[:, columns] + dot(wide[...], tall[:, columns], NN)


def kernel_l0(later, own, late, rest, vrow, vcol, acc, out, amp_a, tall, other, right, wide, sem):
    cut = rest.shape[0]
    fetch(other, sem, [("special", late), ("plain", rest)])
    put_wide(right, other[...])
    put_tall(tall, other[...])
    total, weight = later[2:3, 0:1], later[3:4, 0:1]
    amp = overlap(own, right) / (total - vcol[...] - vrow[:, 0:cut])
    amp_a[...] = amp
    inner = amp[0:cut]
    put_wide(wide, (2.0 * inner - inner.T) * weight)
    for columns in column_blocks(acc.shape[1]):
        out[0:cut, columns] = acc[0:cut, columns] + dot(wide[...], tall[:, columns], NN)
    out[cut:] = acc[cut:]


def kernel_l1(
    later, own, late, rest, vrow, vcol, acc, amp_a, tall_a,
    out, right, tall, wide_ab, wide_ba, wide_bb, result, out_sems,
):
    cut = amp_a.shape[1]
    other = jnp.where(case("special"), late[...], rest[...])
    put_wide(right, other)
    put_tall(tall, other)
    total, weight = later[2:3, 0:1], later[3:4, 0:1]
    amp = overlap(own, right) / (total - vcol[...] - vrow[:, cut:])
    across = amp_a[cut:]
    put_wide(wide_ab, (2.0 * amp[0:cut] - across.T) * weight)
    put_wide(wide_ba, (2.0 * across - amp[0:cut].T) * weight)
    put_wide(wide_bb, (2.0 * amp[cut:] - amp[cut:].T) * weight)
    copies = []
    for i, columns in enumerate(column_blocks(acc.shape[1])):
        result[0:cut, columns] = acc[0:cut, columns] + dot(wide_ab[...], tall[:, columns], NN)
        result[cut:, columns] = (
            acc[cut:, columns]
            + dot(wide_ba[...], tall_a[:, columns], NN)
            + dot(wide_bb[...], tall[:, columns], NN)
        )
        copies.append(pltpu.make_async_copy(result.at[:, columns], out.at[:, columns], out_sems.at[i]))
        copies[-1].start()
    for copy in copies:
        copy.wait()


SMEM = pl.BlockSpec(memory_space=pltpu.SMEM)
VMEM = pl.BlockSpec(memory_space=pltpu.VMEM)
ANY = pl.BlockSpec(memory_space=pl.ANY)


def call(kernel, operands, outs, scratch, flops, limit=None, out_specs=None):
    return pl.pallas_call(
        kernel,
        out_shape=[jax.ShapeDtypeStruct(shape, dtype) for shape, dtype in outs],
        in_specs=[spec for spec, _ in operands],
        out_specs=out_specs or [VMEM] * len(outs),
        scratch_shapes=scratch,
        cost_estimate=pl.CostEstimate(flops=flops, bytes_accessed=8_000_000, transcendentals=0),
        compiler_params=pltpu.CompilerParams(vmem_limit_bytes=limit),
    )(*[value for _, value in operands])


def piece(array, start, size):
    def kernel(source, out, sem):
        copy = pltpu.make_async_copy(source.at[pl.ds(start, size)], out, sem)
        copy.start()
        copy.wait()

    shape = (size, array.shape[1])
    return call(kernel, [(ANY, array)], [(shape, array.dtype)], [pltpu.SemaphoreType.DMA], 0, 4_000_000)[0]


def after(values, token):
    *values, token = lax.optimization_barrier((*values, token))
    return values, token


def body(slices, occ_energy, virt_energy, order, near_keep, far_keep):
    n = lax.axis_size("orb")
    m = n // 2
    specials = (0, m - 1, m, n - 1)
    mates = [(i, i ^ 1) for i in range(n)]
    outers = both_ways([(i, i + 1) for i in range(1, n - 1, 2) if i not in specials])
    straight = both_ways([(0, m), (m - 1, n - 1)])
    opposites = [(i, (i + m) % n) for i in range(n) if i not in specials]
    forwards = both_ways([(0, m - 1), (m, n - 1)])

    own = slices[0]
    rows, k = own.shape
    cut = rows // 5 * 3
    size = rows - cut
    bf16, f32 = jnp.bfloat16, jnp.float32
    pieces = (piece(own, 0, cut), piece(own, cut, size))
    v = [(VMEM, virt_energy[None, :]), (VMEM, virt_energy[:, None])]
    flops = 12 * rows * rows * k

    prev_near = permute(near_keep.astype(f32), [(i, (i + 1) % n) for i in range(n)])
    straight_slices = [permute(pieces[0], straight), permute(pieces[1], straight)]
    mate = permute(own, mates)
    outer = permute(own, outers)
    small = [(SMEM, x) for x in (order, occ_energy, near_keep, prev_near, far_keep)]

    right = pltpu.VMEM((rows, 3 * k), bf16)
    wide = pltpu.VMEM((rows, 3 * rows), bf16)
    tall = pltpu.VMEM((3 * rows, k), bf16)
    dma = pltpu.SemaphoreType.DMA
    acc, own_three = call(
        kernel_d, [small[0], small[1], (VMEM, own), *v],
        [((rows, k), f32), ((rows, 3 * k), bf16)], [right, wide, tall], flops,
    )
    (first, whole), acc = after((straight_slices[1], own), acc)
    late1 = permute(first, forwards)
    pieces = (whole[:cut], whole[cut:])
    rest = [permute(piece, opposites) for piece in pieces]
    late = [permute(straight_slices[0], forwards), late1]
    acc, later = call(
        lambda *refs: kernel_ab("A", *refs),
        [*small, (VMEM, own_three), (VMEM, mate), *v, (VMEM, acc)],
        [((rows, k), f32), ((8, 128), f32)], [right, wide, tall], flops,
    )
    (acc,) = call(
        lambda *refs: kernel_ab("B", *refs),
        [(VMEM, later), (VMEM, own_three), (ANY, outer), *((ANY, x) for x in straight_slices), *v, (VMEM, acc)],
        [((rows, k), f32)], [pltpu.VMEM((rows, k), f32), right, wide, tall, dma], flops,
    )
    acc, amp_a, tall_a = call(
        kernel_l0,
        [(VMEM, later), (VMEM, own_three), (ANY, late[0]), (ANY, rest[0]), *v, (VMEM, acc)],
        [((rows, k), f32), ((rows, cut), f32), ((3 * cut, k), bf16)],
        [pltpu.VMEM((cut, k), f32), pltpu.VMEM((cut, 3 * k), bf16), pltpu.VMEM((cut, 3 * cut), bf16), dma],
        flops // 2,
        26_000_000,
    )
    (acc,) = call(
        kernel_l1,
        [(VMEM, later), (VMEM, own_three), (VMEM, late[1]), (VMEM, rest[1]), *v, (VMEM, acc), (VMEM, amp_a), (VMEM, tall_a)],
        [((rows, k), f32)],
        [
            pltpu.VMEM((size, 3 * k), bf16),
            pltpu.VMEM((3 * size, k), bf16),
            pltpu.VMEM((cut, 3 * size), bf16),
            pltpu.VMEM((size, 3 * cut), bf16),
            pltpu.VMEM((size, 3 * size), bf16),
            pltpu.VMEM((rows, k), f32),
            pltpu.SemaphoreType.DMA((4,)),
        ],
        flops // 2,
        26_000_000,
        [ANY],
    )
    return acc[None]


def solution(mesh):
    return jax.shard_map(
        body,
        mesh=mesh,
        in_specs=(
            P(("frag", "orb"), None, None),
            P("frag"),
            P("frag"),
            P("frag"),
            P(("frag", "orb")),
            P("frag"),
        ),
        out_specs=P(("frag", "orb"), None, None),
        check_vma=False,
    )
```

time: 190 us -> 180 us (0.947)
  Pallas kernels: 58.3 us -> 47.3 us
  local copies, waits for them, and re-layouts: 8.27 us -> 10.4 us
    pallas_call x5 -> x7, Pallas kernels: 58.3 us -> 47.3 us  [call(): pl.pallas_call(kernel, out_shape=[jax.ShapeDtypeStruct(shape, dtype) for...]
    unnamed x18 -> x12, local copies, waits for them, and re-layouts: 1.77 us -> 3.86 us
    ppermute x9, starting transfers between devices: 19.5 us -> 17.6 us  [permute(): return lax.ppermute(block, 'orb', pairs)]
  transfers between devices with their start and end apart: 9 -> 9, of which waited for: 2 -> 2; matrix products, arithmetic and copies ran while one was open for 3% -> 4% of each run, Pallas kernels for 26% -> 23%
where the time goes in v2:
time: 180 us; the launch traced here: 179 us
  waiting for transfers between devices  103 us (57%)
  Pallas kernels  47.3 us (26%)
  starting transfers between devices  17.6 us (10%)
  local copies, waits for them, and re-layouts  10.4 us (6%)
    ppermute x9, waiting for transfers between devices, permute(): return lax.ppermute(block, 'orb', pairs)  103 us
    pallas_call x7, Pallas kernels, call(): pl.pallas_call(kernel, out_shape=[jax.ShapeDtypeStruct(shape, dtype) for...  47.3 us
    ppermute x9, starting transfers between devices, permute(): return lax.ppermute(block, 'orb', pairs)  17.6 us
    slice x2, local copies, waits for them, and re-layouts, body(): pieces = (whole[:cut], whole[cut:])  5.08 us
    unnamed x12, local copies, waits for them, and re-layouts  3.86 us
  transfers between devices with their start and end apart: 9, of which 2 were waited for; matrix products, arithmetic and copies ran while one was open for 4% of the time, Pallas kernels for 23%

profile of v2, /device:TPU:0, one launch (start us, length us, event | category | flops | bytes accessed | tf_op | source)
XLA Modules:
  0.0 179.2 jit_solution(16496012421207829429)
XLA Ops:
  0.0 0.5 collective-permute-start.1
  0.5 1.4 shard_map.67
  1.9 5.5 %collective-permute-start.5 = (f32[384,1024]{1,0:T(8,128)S(1)}, f32[384,1024]{1,0:T(8,128)}, u32[]{:S(2)}, u32[]{:S(2)}) collective-permute-start(f32[384,1024]{1,0:T(8,128)S(1)} %shard_map.67), channel_id=1, source_target_pairs={{0,8},{7,15},{8,0},{15,7},{16,24},{23,31},{24,16},{31,23}} | collective-permute-start | bytes 4718600 | tf_op jit(solution)/shard_map/ppermute | solution.py:14
  7.4 2.2 %collective-permute-start.8 = (f32[640,1024]{1,0:T(8,128)}, f32[640,1024]{1,0:T(8,128)}, u32[]{:S(2)}, u32[]{:S(2)}) collective-permute-start(f32[640,1024]{1,0:T(8,128)} %bitcast.own.source), channel_id=1, source_target_pairs={{1,2},{3,4},{5,6},{9,10},{11,12},{13,14},{2,1},{4,3},{6,5},{10,9},... | collective-permute-start | bytes 7864328 | tf_op jit(solution)/shard_map/ppermute | solution.py:14
  9.6 1.2 shard_map.65
  10.9 1.9 %collective-permute-start.2 = (f32[256,1024]{1,0:T(8,128)S(1)}, f32[256,1024]{1,0:T(8,128)}, u32[]{:S(2)}, u32[]{:S(2)}) collective-permute-start(f32[256,1024]{1,0:T(8,128)S(1)} %shard_map.65), channel_id=1, source_target_pairs={{0,8},{7,15},{8,0},{15,7},{16,24},{23,31},{24,16},{31,23}} | collective-permute-start | bytes 3145736 | tf_op jit(solution)/shard_map/ppermute | solution.py:14
  12.8 0.9 broadcast_in_dim.12.vcol.refs_8_.refs_6_
  13.7 0.6 broadcast_in_dim.9.vrow.refs_7_.refs_5_
  14.3 9.4 %shard_map.64 = (f32[640,1024]{1,0:T(8,128)}, bf16[640,3072]{1,0:T(8,128)(2,1)}) custom-call(s32[16]{0:T(128)} %refs_0_.1, f32[16]{0:T(128)} %refs_1_.1, f32[640,1024]{1,0:T(8,128)} %bitcast.own.source, f32[1,640]{1,0:T(1,128)} %broadcast_in_dim.9.vrow.refs_7_.refs_5_, f32[640,1]{1,0:T(8,128)} %broadcast_in_dim.12.vcol.refs_8_.refs_6_), custom_call_target="tpu_custom_call" | custom-call | flops 5033164800 | bytes 8000000 | tf_op jit(solution)/shard_map/pallas_call | solution.py:189
  23.7 76.4 %collective-permute-done.2.refs_4_ = f32[256,1024]{1,0:T(8,128)} collective-permute-done((f32[256,1024]{1,0:T(8,128)S(1)}, f32[256,1024]{1,0:T(8,128)}, u32[]{:S(2)}, u32[]{:S(2)}) %collective-permute-start.2) | collective-permute-done | bytes 1048608 | tf_op jit(solution)/shard_map/ppermute | solution.py:14
  100.0 2.8 %slice.7 = f32[384,1024]{1,0:T(8,128)} slice(f32[640,1024]{1,0:T(8,128)} %bitcast.own.source), slice={[0:384], [0:1024]} | slice | bytes 3145728 | tf_op jit(solution)/shard_map/slice | solution.py:250
  102.8 0.7 collective-permute-start.7
  103.5 3.0 %collective-permute-start.6 = (f32[384,1024]{1,0:T(8,128)}, f32[384,1024]{1,0:T(8,128)}, u32[]{:S(2)}, u32[]{:S(2)}) collective-permute-start(f32[384,1024]{1,0:T(8,128)} %collective-permute-done.5.refs_3_), channel_id=1, source_target_pairs={{0,7},{8,15},{7,0},{15,8},{16,23},{24,31},{23,16},{31,24}} | collective-permute-start | bytes 4718600 | tf_op jit(solution)/shard_map/ppermute | solution.py:14
  107.2 0.9 collective-permute-start
  108.1 2.3 %slice.6 = f32[256,1024]{1,0:T(8,128)} slice(f32[640,1024]{1,0:T(8,128)} %bitcast.own.source), slice={[384:640], [0:1024]} | slice | bytes 2097152 | tf_op jit(solution)/shard_map/slice | solution.py:250
  110.4 26.5 %collective-permute-done.refs_3_ = f32[1]{0:T(128)} collective-permute-done((f32[1]{0:T(128)}, f32[1]{0:T(128)}, u32[]{:S(2)}, u32[]{:S(2)}) %collective-permute-start) | collective-permute-done | bytes 36 | tf_op jit(solution)/shard_map/ppermute | solution.py:14
  137.0 0.7 collective-permute-start.4
  137.7 2.1 %collective-permute-start.3 = (f32[256,1024]{1,0:T(8,128)}, f32[256,1024]{1,0:T(8,128)}, u32[]{:S(2)}, u32[]{:S(2)}) collective-permute-start(f32[256,1024]{1,0:T(8,128)} %collective-permute-done.2.refs_4_), channel_id=1, source_target_pairs={{0,7},{8,15},{7,0},{15,8},{16,23},{24,31},{23,16},{31,24}} | collective-permute-start | bytes 3145736 | tf_op jit(solution)/shard_map/ppermute | solution.py:14
  139.8 11.9 %shard_map.66 = (f32[640,1024]{1,0:T(8,128)}, f32[8,128]{1,0:T(8,128)}) custom-call(s32[16]{0:T(128)} %refs_0_.1, f32[16]{0:T(128)} %refs_1_.1, s32[1]{0:T(128)S(6)} %copy.12.refs_2_, f32[1]{0:T(128)} %collective-permute-done.refs_3_, s32[8]{0:T(128)} %refs_4_.1, bf16[640,3072]{1,0:T(8,128)(2,1)} %get-tuple-element.15.refs_5_.refs_1_.own, ...), custom_call_target="tpu_custom_call" | custom-call | flops 5033164800 | bytes 8000000 | tf_op jit(solution)/shard_map/pallas_call | solution.py:189
  151.7 13.2 %shard_map.68.acc = f32[640,1024]{1,0:T(8,128)} custom-call(f32[8,128]{1,0:T(8,128)} %get-tuple-element.18.refs_0_.later, bf16[640,3072]{1,0:T(8,128)(2,1)} %get-tuple-element.15.refs_5_.refs_1_.own, f32[640,1024]{1,0:T(8,128)} %collective-permute-done.8.refs_2_, f32[384,1024]{1,0:T(8,128)} %collective-permute-done.5.refs_3_, ...), custom_call_target="tpu_custom_call" | custom-call | flops 5033164800 | bytes 8000000 | tf_op jit(solution)/shard_map/pallas_call | solution.py:189
  165.0 2.1 %copy-done = bf16[640,3072]{1,0:T(8,128)(2,1)S(1)} copy-done((bf16[640,3072]{1,0:T(8,128)(2,1)S(1)}, bf16[640,3072]{1,0:T(8,128)(2,1)}, u32[]{:S(2)}) %copy-start) | copy-done | bytes 3932184
  167.1 1.7 copy-done.2
  168.8 4.7 %shard_map.69 = (f32[640,1024]{1,0:T(8,128)S(1)}, f32[640,384]{1,0:T(8,128)S(1)}, bf16[1152,1024]{1,0:T(8,128)(2,1)S(1)}) custom-call(f32[8,128]{1,0:T(8,128)S(1)} %copy-done.4, bf16[640,3072]{1,0:T(8,128)(2,1)S(1)} %copy-done, f32[384,1024]{1,0:T(8,128)} %collective-permute-done.6.late, f32[384,1024]{1,0:T(8,128)S(1)} %collective-permute-done.7.rest, ...), custom_call_target="tpu_custom_call" | custom-call | flops 2516582400 | bytes 8000000 | tf_op jit(solution)/shard_map/pallas_call | solution.py:189
  173.6 5.5 %shard_map.70 = f32[640,1024]{1,0:T(8,128)} custom-call(f32[8,128]{1,0:T(8,128)S(1)} %copy-done.4, bf16[640,3072]{1,0:T(8,128)(2,1)S(1)} %copy-done, f32[256,1024]{1,0:T(8,128)} %collective-permute-done.3.late, f32[256,1024]{1,0:T(8,128)S(1)} %collective-permute-done.4.rest, f32[1,640]{1,0:T(1,128)S(1)} %copy-done.3, f32[640,1]{1,0:T(8,128)S(1)} %copy-done.1, ...), custom_call_target="tpu_custom_call" | custom-call | flops 2516582400 | bytes 8000000 | tf_op jit(solution)/shard_map/pallas_call | solution.py:189
  (17 shorter events, 0.0 us)
Async XLA Ops:
  0.0 137.7 %collective-permute-start.1 = (f32[640,1024]{1,0:T(8,128)}, f32[640,1024]{1,0:T(8,128)}, u32[]{:S(2)}, u32[]{:S(2)}) collective-permute-start(f32[640,1024]{1,0:T(8,128)} %bitcast.own.source), channel_id=1, source_target_pairs={{0,1},{1,0},{2,3},{3,2},{4,5},{5,4},{6,7},{7,6},{8,9},{9,8},{10,11... | collective-permute-start | bytes 7864328 | tf_op jit(solution)/shard_map/ppermute | solution.py:14
  1.9 10.9 %copy-start.5 = (f32[640]{0:T(1024)S(1)}, f32[640]{0:T(1024)}, u32[]{:S(2)}) copy-start(f32[640]{0:T(1024)} %param.8) | copy-start | bytes 7684
  1.9 101.6 %collective-permute-start.5 = (f32[384,1024]{1,0:T(8,128)S(1)}, f32[384,1024]{1,0:T(8,128)}, u32[]{:S(2)}, u32[]{:S(2)}) collective-permute-start(f32[384,1024]{1,0:T(8,128)S(1)} %shard_map.67), channel_id=1, source_target_pairs={{0,8},{7,15},{8,0},{15,7},{16,24},{23,31},{24,16},{31,23}} | collective-permute-start | bytes 4718600 | tf_op jit(solution)/shard_map/ppermute | solution.py:14
  7.4 144.3 %collective-permute-start.8 = (f32[640,1024]{1,0:T(8,128)}, f32[640,1024]{1,0:T(8,128)}, u32[]{:S(2)}, u32[]{:S(2)}) collective-permute-start(f32[640,1024]{1,0:T(8,128)} %bitcast.own.source), channel_id=1, source_target_pairs={{1,2},{3,4},{5,6},{9,10},{11,12},{13,14},{2,1},{4,3},{6,5},{10,9},... | collective-permute-start | bytes 7864328 | tf_op jit(solution)/shard_map/ppermute | solution.py:14
  10.9 89.2 %collective-permute-start.2 = (f32[256,1024]{1,0:T(8,128)S(1)}, f32[256,1024]{1,0:T(8,128)}, u32[]{:S(2)}, u32[]{:S(2)}) collective-permute-start(f32[256,1024]{1,0:T(8,128)S(1)} %shard_map.65), channel_id=1, source_target_pairs={{0,8},{7,15},{8,0},{15,7},{16,24},{23,31},{24,16},{31,23}} | collective-permute-start | bytes 3145736 | tf_op jit(solution)/shard_map/ppermute | solution.py:14
  102.8 62.2 %collective-permute-start.7 = (f32[384,1024]{1,0:T(8,128)}, f32[384,1024]{1,0:T(8,128)S(1)}, u32[]{:S(2)}, u32[]{:S(2)}) collective-permute-start(f32[384,1024]{1,0:T(8,128)} %slice.7), channel_id=1, source_target_pairs={{1,9},{2,10},{3,11},{4,12},{5,13},{6,14},{9,1},{10,2},{11,3},{12,4... | collective-permute-start | bytes 4718600 | tf_op jit(solution)/shard_map/ppermute | solution.py:14
  103.5 61.4 %collective-permute-start.6 = (f32[384,1024]{1,0:T(8,128)}, f32[384,1024]{1,0:T(8,128)}, u32[]{:S(2)}, u32[]{:S(2)}) collective-permute-start(f32[384,1024]{1,0:T(8,128)} %collective-permute-done.5.refs_3_), channel_id=1, source_target_pairs={{0,7},{8,15},{7,0},{15,8},{16,23},{24,31},{23,16},{31,24}} | collective-permute-start | bytes 4718600 | tf_op jit(solution)/shard_map/ppermute | solution.py:14
  107.2 29.8 %collective-permute-start = (f32[1]{0:T(128)}, f32[1]{0:T(128)}, u32[]{:S(2)}, u32[]{:S(2)}) collective-permute-start(f32[1]{0:T(128)} %convert_element_type.3), channel_id=1, source_target_pairs={{0,1},{1,2},{2,3},{3,4},{4,5},{5,6},{6,7},{7,8},{8,9},{9,10},{10,1... | collective-permute-start | bytes 20 | tf_op jit(solution)/shard_map/ppermute | solution.py:14
  137.0 36.6 %collective-permute-start.4 = (f32[256,1024]{1,0:T(8,128)}, f32[256,1024]{1,0:T(8,128)S(1)}, u32[]{:S(2)}, u32[]{:S(2)}) collective-permute-start(f32[256,1024]{1,0:T(8,128)} %slice.6), channel_id=1, source_target_pairs={{1,9},{2,10},{3,11},{4,12},{5,13},{6,14},{9,1},{10,2},{11,3},{12,4... | collective-permute-start | bytes 3145736 | tf_op jit(solution)/shard_map/ppermute | solution.py:14
  137.7 35.9 %collective-permute-start.3 = (f32[256,1024]{1,0:T(8,128)}, f32[256,1024]{1,0:T(8,128)}, u32[]{:S(2)}, u32[]{:S(2)}) collective-permute-start(f32[256,1024]{1,0:T(8,128)} %collective-permute-done.2.refs_4_), channel_id=1, source_target_pairs={{0,7},{8,15},{7,0},{15,8},{16,23},{24,31},{23,16},{31,24}} | collective-permute-start | bytes 3145736 | tf_op jit(solution)/shard_map/ppermute | solution.py:14
  151.7 13.2 %copy-start.1 = (f32[640,1]{1,0:T(8,128)S(1)}, f32[640,1]{1,0:T(8,128)}, u32[]{:S(2)}) copy-start(f32[640,1]{1,0:T(8,128)} %broadcast_in_dim.12.vcol.refs_8_.refs_6_) | copy-start | bytes 7684
  151.7 13.2 %copy-start.3 = (f32[1,640]{1,0:T(1,128)S(1)}, f32[1,640]{1,0:T(1,128)}, u32[]{:S(2)}) copy-start(f32[1,640]{1,0:T(1,128)} %broadcast_in_dim.9.vrow.refs_7_.refs_5_) | copy-start | bytes 7684
  151.7 13.2 %copy-start.4 = (f32[8,128]{1,0:T(8,128)S(1)}, f32[8,128]{1,0:T(8,128)}, u32[]{:S(2)}) copy-start(f32[8,128]{1,0:T(8,128)} %get-tuple-element.18.refs_0_.later) | copy-start | bytes 12292
  165.0 2.1 %copy-start = (bf16[640,3072]{1,0:T(8,128)(2,1)S(1)}, bf16[640,3072]{1,0:T(8,128)(2,1)}, u32[]{:S(2)}) copy-start(bf16[640,3072]{1,0:T(8,128)(2,1)} %get-tuple-element.15.refs_5_.refs_1_.own) | copy-start | bytes 11796484
  167.1 1.7 copy-start.2

commit v3 on v2

--- a/solution.py
+++ b/solution.py
@@ -137,11 +137,12 @@
         out[:, columns] = acc[:, columns] + dot(wide[...], tall[:, columns], NN)
 
 
-def kernel_l0(later, own, late, rest, vrow, vcol, acc, out, amp_a, tall, other, right, wide, sem):
+def kernel_l0(later, own, late0, late1, rest, vrow, vcol, acc, out, amp_a, tall, right, wide):
     cut = rest.shape[0]
-    fetch(other, sem, [("special", late), ("plain", rest)])
-    put_wide(right, other[...])
-    put_tall(tall, other[...])
+    late = jnp.concatenate([late0[...], late1[0 : cut - late0.shape[0]]], axis=0)
+    other = jnp.where(case("special"), late, rest[...])
+    put_wide(right, other)
+    put_tall(tall, other)
     total, weight = later[2:3, 0:1], later[3:4, 0:1]
     amp = overlap(own, right) / (total - vcol[...] - vrow[:, 0:cut])
     amp_a[...] = amp
@@ -157,7 +158,8 @@
     out, right, tall, wide_ab, wide_ba, wide_bb, result, out_sems,
 ):
     cut = amp_a.shape[1]
-    other = jnp.where(case("special"), late[...], rest[...])
+    size = rest.shape[0]
+    other = jnp.where(case("special"), late[late.shape[0] - size :], rest[...])
     put_wide(right, other)
     put_tall(tall, other)
     total, weight = later[2:3, 0:1], later[3:4, 0:1]
@@ -224,10 +226,11 @@
 
     own = slices[0]
     rows, k = own.shape
-    cut = rows // 5 * 3
+    cut = rows // 5 * 4
+    cut_special = rows // 5 * 3
     size = rows - cut
     bf16, f32 = jnp.bfloat16, jnp.float32
-    pieces = (piece(own, 0, cut), piece(own, cut, size))
+    pieces = (piece(own, 0, cut_special), piece(own, cut_special, rows - cut_special))
     v = [(VMEM, virt_energy[None, :]), (VMEM, virt_energy[:, None])]
     flops = 12 * rows * rows * k
 
@@ -243,28 +246,29 @@
     dma = pltpu.SemaphoreType.DMA
     acc, own_three = call(
         kernel_d, [small[0], small[1], (VMEM, own), *v],
-        [((rows, k), f32), ((rows, 3 * k), bf16)], [right, wide, tall], flops,
-    )
-    (first, whole), acc = after((straight_slices[1], own), acc)
+        [((rows, k), f32), ((rows, 3 * k), bf16)], [right, wide, tall], flops, 40_000_000,
+    )
+    (first,), acc = after((straight_slices[1],), acc)
     late1 = permute(first, forwards)
+    acc, later = call(
+        lambda *refs: kernel_ab("A", *refs),
+        [*small, (VMEM, own_three), (VMEM, mate), *v, (VMEM, acc)],
+        [((rows, k), f32), ((8, 128), f32)], [right, wide, tall], flops, 40_000_000,
+    )
+    (whole,), acc = after((own,), acc)
     pieces = (whole[:cut], whole[cut:])
     rest = [permute(piece, opposites) for piece in pieces]
     late = [permute(straight_slices[0], forwards), late1]
-    acc, later = call(
-        lambda *refs: kernel_ab("A", *refs),
-        [*small, (VMEM, own_three), (VMEM, mate), *v, (VMEM, acc)],
-        [((rows, k), f32), ((8, 128), f32)], [right, wide, tall], flops,
-    )
     (acc,) = call(
         lambda *refs: kernel_ab("B", *refs),
         [(VMEM, later), (VMEM, own_three), (ANY, outer), *((ANY, x) for x in straight_slices), *v, (VMEM, acc)],
-        [((rows, k), f32)], [pltpu.VMEM((rows, k), f32), right, wide, tall, dma], flops,
+        [((rows, k), f32)], [pltpu.VMEM((rows, k), f32), right, wide, tall, dma], flops, 40_000_000,
     )
     acc, amp_a, tall_a = call(
         kernel_l0,
-        [(VMEM, later), (VMEM, own_three), (ANY, late[0]), (ANY, rest[0]), *v, (VMEM, acc)],
+        [(VMEM, later), (VMEM, own_three), (VMEM, late[0]), (VMEM, late[1]), (VMEM, rest[0]), *v, (VMEM, acc)],
         [((rows, k), f32), ((rows, cut), f32), ((3 * cut, k), bf16)],
-        [pltpu.VMEM((cut, k), f32), pltpu.VMEM((cut, 3 * k), bf16), pltpu.VMEM((cut, 3 * cut), bf16), dma],
+        [pltpu.VMEM((cut, 3 * k), bf16), pltpu.VMEM((cut, 3 * cut), bf16)],
         flops // 2,
         26_000_000,
     )

time: 180 us -> 154 us (0.86)
  the two profiles are of different devices: /device:TPU:0 before, /device:TPU:3 now
where the time goes in v3:
time: 154 us
  starting transfers between devices  95.3 us (62%)
  Pallas kernels  31.8 us (21%)
  waiting for transfers between devices  22.8 us (15%)
  local copies, waits for them, and re-layouts  2.98 us (2%)
    ppermute x9, starting transfers between devices, permute(): return lax.ppermute(block, 'orb', pairs)  95.3 us
    pallas_call x7, Pallas kernels, call(): pl.pallas_call(kernel, out_shape=[jax.ShapeDtypeStruct(shape, dtype) for...  31.8 us
    ppermute x9, waiting for transfers between devices, permute(): return lax.ppermute(block, 'orb', pairs)  22.8 us
  transfers between devices with their start and end apart: 9, of which 2 were waited for; matrix products, arithmetic and copies ran while one was open for 2% of the time, Pallas kernels for 18%

profile of v3, /device:TPU:3, one launch (start us, length us, event | category | flops | bytes accessed | tf_op | source)
XLA Modules:
  0.0 154.0 jit_solution(13948029010066353743)
XLA Ops:
  0.0 0.7 collective-permute-start.1
  0.7 1.2 shard_map.65
  1.9 0.0 copy-start
  1.9 0.0 copy-start.1
  2.0 0.9 collective-permute-start.2
  2.8 1.4 shard_map.67
  4.2 0.8 collective-permute-start.5
  5.0 3.1 %collective-permute-start.8 = (f32[640,1024]{1,0:T(8,128)}, f32[640,1024]{1,0:T(8,128)S(1)}, u32[]{:S(2)}, u32[]{:S(2)}) collective-permute-start(f32[640,1024]{1,0:T(8,128)} %bitcast.own.source), channel_id=1, source_target_pairs={{1,2},{3,4},{5,6},{9,10},{11,12},{13,14},{2,1},{4,3},{6,5},{10,9},... | collective-permute-start | bytes 7864328 | tf_op jit(solution)/shard_map/ppermute | solution.py:14
  8.7 28.3 %collective-permute-start = (f32[1]{0:T(128)}, f32[1]{0:T(128)}, u32[]{:S(2)}, u32[]{:S(2)}) collective-permute-start(f32[1]{0:T(128)} %convert_element_type.3), channel_id=1, source_target_pairs={{0,1},{1,2},{2,3},{3,4},{4,5},{5,6},{6,7},{7,8},{8,9},{9,10},{10,1... | collective-permute-start | bytes 20 | tf_op jit(solution)/shard_map/ppermute | solution.py:14
  37.0 0.1 broadcast_in_dim.12.vcol.refs_8_.refs_6_
  37.2 0.0 copy-start.2
  37.2 7.9 %shard_map.64 = (f32[640,1024]{1,0:T(8,128)S(1)}, bf16[640,3072]{1,0:T(8,128)(2,1)S(1)}) custom-call(s32[16]{0:T(128)S(1)} %copy-done, f32[16]{0:T(128)S(1)} %copy-done.1, f32[640,1024]{1,0:T(8,128)} %bitcast.own.source, f32[1,640]{1,0:T(1,128)S(1)} %broadcast_in_dim.9.vrow.refs_7_.refs_5_, f32[640,1]{1,0:T(8,128)S(1)} %broadcast_in_dim.12.vcol.refs_8_.refs_6_), custom_call_target="tpu_custom_call" | custom-call | flops 5033164800 | bytes 8000000 | tf_op jit(solution)/shard_map/pallas_call | solution.py:191
  45.2 7.3 %shard_map.66 = (f32[640,1024]{1,0:T(8,128)S(1)}, f32[8,128]{1,0:T(8,128)S(1)}) custom-call(s32[16]{0:T(128)S(1)} %copy-done, f32[16]{0:T(128)S(1)} %copy-done.1, s32[1]{0:T(128)S(6)} %copy.12.refs_2_, f32[1]{0:T(128)} %collective-permute-done.refs_3_, s32[8]{0:T(128)S(1)} %copy-done.2, bf16[640,3072]{1,0:T(8,128)(2,1)S(1)} %get-tuple-element.16.refs_5_.refs_1_.own, ...), custom_call_target="tpu_custom_call" | custom-call | flops 5033164800 | bytes 8000000 | tf_op jit(solution)/shard_map/pallas_call | solution.py:191
  52.5 1.7 %slice.7 = f32[512,1024]{1,0:T(8,128)S(1)} slice(f32[640,1024]{1,0:T(8,128)} %bitcast.own.source), slice={[0:512], [0:1024]} | slice | bytes 4194304 | tf_op jit(solution)/shard_map/slice | solution.py:259
  54.2 58.2 %collective-permute-start.7 = (f32[512,1024]{1,0:T(8,128)S(1)}, f32[512,1024]{1,0:T(8,128)S(1)}, u32[]{:S(2)}, u32[]{:S(2)}) collective-permute-start(f32[512,1024]{1,0:T(8,128)S(1)} %slice.7), channel_id=1, source_target_pairs={{1,9},{2,10},{3,11},{4,12},{5,13},{6,14},{9,1},{10,2},{11,3},{12,4... | collective-permute-start | bytes 6291464 | tf_op jit(solution)/shard_map/ppermute | solution.py:14
  112.5 0.8 collective-permute-start.6
  113.2 0.7 collective-permute-start.3
  114.0 1.1 slice.6
  115.0 1.9 %collective-permute-start.4 = (f32[128,1024]{1,0:T(8,128)S(1)}, f32[128,1024]{1,0:T(8,128)S(1)}, u32[]{:S(2)}, u32[]{:S(2)}) collective-permute-start(f32[128,1024]{1,0:T(8,128)S(1)} %slice.6), channel_id=1, source_target_pairs={{1,9},{2,10},{3,11},{4,12},{5,13},{6,14},{9,1},{10,2},{11,3},{12,4... | collective-permute-start | bytes 1572872 | tf_op jit(solution)/shard_map/ppermute | solution.py:14
  117.0 6.4 %shard_map.68.acc = f32[640,1024]{1,0:T(8,128)S(1)} custom-call(f32[8,128]{1,0:T(8,128)S(1)} %get-tuple-element.19.refs_0_.later, bf16[640,3072]{1,0:T(8,128)(2,1)S(1)} %get-tuple-element.16.refs_5_.refs_1_.own, f32[640,1024]{1,0:T(8,128)S(1)} %collective-permute-done.8.refs_2_, f32[384,1024]{1,0:T(8,128)S(1)} %collective-permute-done.5.refs_3_, ...), custom_call_target="tpu_custom_call" | custom-call | flops 5033164800 | bytes 8000000 | tf_op jit(solution)/shard_map/pallas_call | solution.py:191
  123.4 21.4 %collective-permute-done.7.rest = f32[512,1024]{1,0:T(8,128)S(1)} collective-permute-done((f32[512,1024]{1,0:T(8,128)S(1)}, f32[512,1024]{1,0:T(8,128)S(1)}, u32[]{:S(2)}, u32[]{:S(2)}) %collective-permute-start.7) | collective-permute-done | bytes 2097184 | tf_op jit(solution)/shard_map/ppermute | solution.py:14
  144.7 4.2 %shard_map.69 = (f32[640,1024]{1,0:T(8,128)S(1)}, f32[640,512]{1,0:T(8,128)S(1)}, bf16[1536,1024]{1,0:T(8,128)(2,1)S(1)}) custom-call(f32[8,128]{1,0:T(8,128)S(1)} %get-tuple-element.19.refs_0_.later, bf16[640,3072]{1,0:T(8,128)(2,1)S(1)} %get-tuple-element.16.refs_5_.refs_1_.own, f32[384,1024]{1,0:T(8,128)S(1)} %collective-permute-done.6.late0, ...), custom_call_target="tpu_custom_call" | custom-call | flops 2516582400 | bytes 8000000 | tf_op jit(solution)/shard_map/pallas_call | solution.py:191
  148.9 1.5 collective-permute-done.4.rest
  150.4 3.4 %shard_map.70 = f32[640,1024]{1,0:T(8,128)} custom-call(f32[8,128]{1,0:T(8,128)S(1)} %get-tuple-element.19.refs_0_.later, bf16[640,3072]{1,0:T(8,128)(2,1)S(1)} %get-tuple-element.16.refs_5_.refs_1_.own, f32[256,1024]{1,0:T(8,128)S(1)} %collective-permute-done.3.late1.late, f32[128,1024]{1,0:T(8,128)S(1)} %collective-permute-done.4.rest, ...), custom_call_target="tpu_custom_call" | custom-call | flops 2516582400 | bytes 8000000 | tf_op jit(solution)/shard_map/pallas_call | solution.py:191
  (13 shorter events, 0.0 us)
Async XLA Ops:
  0.0 45.1 %collective-permute-start.1 = (f32[640,1024]{1,0:T(8,128)}, f32[640,1024]{1,0:T(8,128)S(1)}, u32[]{:S(2)}, u32[]{:S(2)}) collective-permute-start(f32[640,1024]{1,0:T(8,128)} %bitcast.own.source), channel_id=1, source_target_pairs={{0,1},{1,0},{2,3},{3,2},{4,5},{5,4},{6,7},{7,6},{8,9},{9,8},{10,11... | collective-permute-start | bytes 7864328 | tf_op jit(solution)/shard_map/ppermute | solution.py:14
  1.9 35.1 %copy-start.3 = (f32[640]{0:T(1024)S(1)}, f32[640]{0:T(1024)}, u32[]{:S(2)}) copy-start(f32[640]{0:T(1024)} %param.8) | copy-start | bytes 7684
  1.9 35.3 %copy-start = (s32[16]{0:T(128)S(1)}, s32[16]{0:T(128)}, u32[]{:S(2)}) copy-start(s32[16]{0:T(128)} %refs_0_.1) | copy-start | bytes 196
  1.9 35.3 %copy-start.1 = (f32[16]{0:T(128)S(1)}, f32[16]{0:T(128)}, u32[]{:S(2)}) copy-start(f32[16]{0:T(128)} %refs_1_.1) | copy-start | bytes 196
  2.0 43.2 %collective-permute-start.2 = (f32[256,1024]{1,0:T(8,128)S(1)}, f32[256,1024]{1,0:T(8,128)S(1)}, u32[]{:S(2)}, u32[]{:S(2)}) collective-permute-start(f32[256,1024]{1,0:T(8,128)S(1)} %shard_map.65), channel_id=1, source_target_pairs={{0,8},{7,15},{8,0},{15,7},{16,24},{23,31},{24,16},{31,23}} | collective-permute-start | bytes 3145736 | tf_op jit(solution)/shard_map/ppermute | solution.py:14
  4.2 108.2 %collective-permute-start.5 = (f32[384,1024]{1,0:T(8,128)S(1)}, f32[384,1024]{1,0:T(8,128)S(1)}, u32[]{:S(2)}, u32[]{:S(2)}) collective-permute-start(f32[384,1024]{1,0:T(8,128)S(1)} %shard_map.67), channel_id=1, source_target_pairs={{0,8},{7,15},{8,0},{15,7},{16,24},{23,31},{24,16},{31,23}} | collective-permute-start | bytes 4718600 | tf_op jit(solution)/shard_map/ppermute | solution.py:14
  5.0 112.0 %collective-permute-start.8 = (f32[640,1024]{1,0:T(8,128)}, f32[640,1024]{1,0:T(8,128)S(1)}, u32[]{:S(2)}, u32[]{:S(2)}) collective-permute-start(f32[640,1024]{1,0:T(8,128)} %bitcast.own.source), channel_id=1, source_target_pairs={{1,2},{3,4},{5,6},{9,10},{11,12},{13,14},{2,1},{4,3},{6,5},{10,9},... | collective-permute-start | bytes 7864328 | tf_op jit(solution)/shard_map/ppermute | solution.py:14
  8.7 36.4 %collective-permute-start = (f32[1]{0:T(128)}, f32[1]{0:T(128)}, u32[]{:S(2)}, u32[]{:S(2)}) collective-permute-start(f32[1]{0:T(128)} %convert_element_type.3), channel_id=1, source_target_pairs={{0,1},{1,2},{2,3},{3,4},{4,5},{5,6},{6,7},{7,8},{8,9},{9,10},{10,1... | collective-permute-start | bytes 20 | tf_op jit(solution)/shard_map/ppermute | solution.py:14
  37.2 7.9 %copy-start.2 = (s32[8]{0:T(128)S(1)}, s32[8]{0:T(128)}, u32[]{:S(2)}) copy-start(s32[8]{0:T(128)} %refs_4_.1) | copy-start | bytes 100
  54.2 90.5 %collective-permute-start.7 = (f32[512,1024]{1,0:T(8,128)S(1)}, f32[512,1024]{1,0:T(8,128)S(1)}, u32[]{:S(2)}, u32[]{:S(2)}) collective-permute-start(f32[512,1024]{1,0:T(8,128)S(1)} %slice.7), channel_id=1, source_target_pairs={{1,9},{2,10},{3,11},{4,12},{5,13},{6,14},{9,1},{10,2},{11,3},{12,4... | collective-permute-start | bytes 6291464 | tf_op jit(solution)/shard_map/ppermute | solution.py:14
  112.5 10.9 %collective-permute-start.6 = (f32[384,1024]{1,0:T(8,128)S(1)}, f32[384,1024]{1,0:T(8,128)S(1)}, u32[]{:S(2)}, u32[]{:S(2)}) collective-permute-start(f32[384,1024]{1,0:T(8,128)S(1)} %collective-permute-done.5.refs_3_), channel_id=1, source_target_pairs={{0,7},{8,15},{7,0},{15,8},{16,23},{24,31},{23,16},{31,24}} | collective-permute-start | bytes 4718600 | tf_op jit(solution)/shard_map/ppermute | solution.py:14
  113.2 10.2 %collective-permute-start.3 = (f32[256,1024]{1,0:T(8,128)S(1)}, f32[256,1024]{1,0:T(8,128)S(1)}, u32[]{:S(2)}, u32[]{:S(2)}) collective-permute-start(f32[256,1024]{1,0:T(8,128)S(1)} %collective-permute-done.2.refs_4_), channel_id=1, source_target_pairs={{0,7},{8,15},{7,0},{15,8},{16,23},{24,31},{23,16},{31,24}} | collective-permute-start | bytes 3145736 | tf_op jit(solution)/shard_map/ppermute | solution.py:14
  115.0 35.3 %collective-permute-start.4 = (f32[128,1024]{1,0:T(8,128)S(1)}, f32[128,1024]{1,0:T(8,128)S(1)}, u32[]{:S(2)}, u32[]{:S(2)}) collective-permute-start(f32[128,1024]{1,0:T(8,128)S(1)} %slice.6), channel_id=1, source_target_pairs={{1,9},{2,10},{3,11},{4,12},{5,13},{6,14},{9,1},{10,2},{11,3},{12,4... | collective-permute-start | bytes 1572872 | tf_op jit(solution)/shard_map/ppermute | solution.py:14

commit v4 on v3

--- a/solution.py
+++ b/solution.py
@@ -6,6 +6,7 @@
 from jax.sharding import PartitionSpec as P
 
 
+EXTRA = 8
 NT = (((1,), (1,)), ((), ()))
 NN = (((1,), (0,)), ((), ()))
 
@@ -22,6 +23,22 @@
     high = x.astype(jnp.bfloat16)
     low = (x - high.astype(jnp.float32)).astype(jnp.bfloat16)
     return high, low
+
+
+def put_tall_turned(ref, x):
+    high, low = split(x.T)
+    k = x.shape[1]
+    ref[0:k] = high
+    ref[k : 2 * k] = low
+    ref[2 * k : 3 * k] = high
+
+
+def put_across(ref, x):
+    high, low = split(x)
+    k = x.shape[1]
+    ref[:, 0:k] = high
+    ref[:, k : 2 * k] = high
+    ref[:, 2 * k : 3 * k] = low
 
 
 def dot(left, right, dims):
@@ -128,7 +145,7 @@
         cut = special0.shape[0]
         fetch(other, sem, [("plain", plain)])
         fetch(other.at[0:cut], sem, [("special", special0)])
-        fetch(other.at[cut:], sem, [("special", special1)])
+        fetch(other.at[cut:], sem, [("special", special1.at[0 : special1.shape[0] - EXTRA])])
     put_wide(right, other[...])
     put_tall(tall, other[...])
     amp = overlap(own, right) / (total - vcol[...] - vrow[...])
@@ -137,13 +154,24 @@
         out[:, columns] = acc[:, columns] + dot(wide[...], tall[:, columns], NN)
 
 
+def kernel_t(own, out):
+    put_tall_turned(out, own[...])
+
+
+def late_scalars(later, late1):
+    n = lax.axis_size("orb")
+    first = lax.rem(lax.axis_index("orb"), n // 2) == 0
+    last = late1.shape[0] - EXTRA
+    return later[2:3, 0:1], jnp.where(first, late1[last : last + 1, 0:1], later[3:4, 0:1])
+
+
 def kernel_l0(later, own, late0, late1, rest, vrow, vcol, acc, out, amp_a, tall, right, wide):
     cut = rest.shape[0]
     late = jnp.concatenate([late0[...], late1[0 : cut - late0.shape[0]]], axis=0)
     other = jnp.where(case("special"), late, rest[...])
     put_wide(right, other)
     put_tall(tall, other)
-    total, weight = later[2:3, 0:1], later[3:4, 0:1]
+    total, weight = late_scalars(later, late1)
     amp = overlap(own, right) / (total - vcol[...] - vrow[:, 0:cut])
     amp_a[...] = amp
     inner = amp[0:cut]
@@ -154,20 +182,21 @@
 
 
 def kernel_l1(
-    later, own, late, rest, vrow, vcol, acc, amp_a, tall_a,
-    out, right, tall, wide_ab, wide_ba, wide_bb, result, out_sems,
+    later, own_turned, late, rest, vrow, vcol, acc, amp_a, tall_a,
+    out, left, tall, wide_ab, wide_ba, wide_bb, result, out_sems,
 ):
     cut = amp_a.shape[1]
     size = rest.shape[0]
-    other = jnp.where(case("special"), late[late.shape[0] - size :], rest[...])
-    put_wide(right, other)
+    last = late.shape[0] - EXTRA
+    other = jnp.where(case("special"), late[last - size : last], rest[...])
+    put_across(left, other)
     put_tall(tall, other)
-    total, weight = later[2:3, 0:1], later[3:4, 0:1]
-    amp = overlap(own, right) / (total - vcol[...] - vrow[:, cut:])
+    total, weight = late_scalars(later, late)
+    turned = dot(left[...], own_turned[...], NN) / (total - vrow[...] - vcol[cut:])
     across = amp_a[cut:]
-    put_wide(wide_ab, (2.0 * amp[0:cut] - across.T) * weight)
-    put_wide(wide_ba, (2.0 * across - amp[0:cut].T) * weight)
-    put_wide(wide_bb, (2.0 * amp[cut:] - amp[cut:].T) * weight)
+    put_wide(wide_ab, ((2.0 * turned[:, 0:cut] - across) * weight).T)
+    put_wide(wide_ba, (2.0 * across - turned[:, 0:cut]) * weight)
+    put_wide(wide_bb, (2.0 * turned[:, cut:].T - turned[:, cut:]) * weight)
     copies = []
     for i, columns in enumerate(column_blocks(acc.shape[1])):
         result[0:cut, columns] = acc[0:cut, columns] + dot(wide_ab[...], tall[:, columns], NN)
@@ -199,14 +228,18 @@
     )(*[value for _, value in operands])
 
 
-def piece(array, start, size):
-    def kernel(source, out, sem):
-        copy = pltpu.make_async_copy(source.at[pl.ds(start, size)], out, sem)
+def piece(array, start, size, tag=None):
+    def kernel(source, *rest):
+        *tags, out, sem = rest
+        copy = pltpu.make_async_copy(source.at[pl.ds(start, size)], out.at[pl.ds(0, size)], sem)
         copy.start()
+        for value in tags:
+            out[size:] = jnp.full((EXTRA, out.shape[1]), value[0], out.dtype)
         copy.wait()
 
-    shape = (size, array.shape[1])
-    return call(kernel, [(ANY, array)], [(shape, array.dtype)], [pltpu.SemaphoreType.DMA], 0, 4_000_000)[0]
+    tags = [] if tag is None else [(SMEM, tag)]
+    shape = (size + EXTRA * len(tags), array.shape[1])
+    return call(kernel, [(ANY, array), *tags], [(shape, array.dtype)], [pltpu.SemaphoreType.DMA], 0, 4_000_000)[0]
 
 
 def after(values, token):
@@ -230,11 +263,12 @@
     cut_special = rows // 5 * 3
     size = rows - cut
     bf16, f32 = jnp.bfloat16, jnp.float32
-    pieces = (piece(own, 0, cut_special), piece(own, cut_special, rows - cut_special))
+    near_weight = near_keep.astype(f32)
+    pieces = (piece(own, 0, cut_special), piece(own, cut_special, rows - cut_special, near_weight))
     v = [(VMEM, virt_energy[None, :]), (VMEM, virt_energy[:, None])]
     flops = 12 * rows * rows * k
 
-    prev_near = permute(near_keep.astype(f32), [(i, (i + 1) % n) for i in range(n)])
+    prev_near = permute(near_weight, [(i, i + 1) for i in range(n) if i not in (m - 1, n - 1)])
     straight_slices = [permute(pieces[0], straight), permute(pieces[1], straight)]
     mate = permute(own, mates)
     outer = permute(own, outers)
@@ -246,14 +280,14 @@
     dma = pltpu.SemaphoreType.DMA
     acc, own_three = call(
         kernel_d, [small[0], small[1], (VMEM, own), *v],
-        [((rows, k), f32), ((rows, 3 * k), bf16)], [right, wide, tall], flops, 40_000_000,
+        [((rows, k), f32), ((rows, 3 * k), bf16)], [right, wide, tall], flops, 32_000_000,
     )
     (first,), acc = after((straight_slices[1],), acc)
     late1 = permute(first, forwards)
     acc, later = call(
         lambda *refs: kernel_ab("A", *refs),
         [*small, (VMEM, own_three), (VMEM, mate), *v, (VMEM, acc)],
-        [((rows, k), f32), ((8, 128), f32)], [right, wide, tall], flops, 40_000_000,
+        [((rows, k), f32), ((8, 128), f32)], [right, wide, tall], flops, 32_000_000,
     )
     (whole,), acc = after((own,), acc)
     pieces = (whole[:cut], whole[cut:])
@@ -262,8 +296,10 @@
     (acc,) = call(
         lambda *refs: kernel_ab("B", *refs),
         [(VMEM, later), (VMEM, own_three), (ANY, outer), *((ANY, x) for x in straight_slices), *v, (VMEM, acc)],
-        [((rows, k), f32)], [pltpu.VMEM((rows, k), f32), right, wide, tall, dma], flops, 40_000_000,
-    )
+        [((rows, k), f32)], [pltpu.VMEM((rows, k), f32), right, wide, tall, dma], flops, 32_000_000,
+    )
+    (whole,), acc = after((own,), acc)
+    (own_turned,) = call(kernel_t, [(VMEM, whole)], [((3 * k, rows), bf16)], [], 0, 20_000_000)
     acc, amp_a, tall_a = call(
         kernel_l0,
         [(VMEM, later), (VMEM, own_three), (VMEM, late[0]), (VMEM, late[1]), (VMEM, rest[0]), *v, (VMEM, acc)],
@@ -274,7 +310,7 @@
     )
     (acc,) = call(
         kernel_l1,
-        [(VMEM, later), (VMEM, own_three), (VMEM, late[1]), (VMEM, rest[1]), *v, (VMEM, acc), (VMEM, amp_a), (VMEM, tall_a)],
+        [(VMEM, later), (VMEM, own_turned), (VMEM, late[1]), (VMEM, rest[1]), *v, (VMEM, acc), (VMEM, amp_a), (VMEM, tall_a)],
         [((rows, k), f32)],
         [
             pltpu.VMEM((size, 3 * k), bf16),

time: 154 us -> 156 us (1.013)
  the two profiles are of different devices: /device:TPU:3 before, /device:TPU:7 now
where the time goes in v4:
time: 156 us; the launch traced here: 155 us
  starting transfers between devices  96.3 us (62%)
  Pallas kernels  33.9 us (22%)
  waiting for transfers between devices  21.3 us (14%)
  local copies, waits for them, and re-layouts  2.98 us (2%)
    ppermute x9, starting transfers between devices, permute(): return lax.ppermute(block, 'orb', pairs)  96.3 us
    pallas_call x8, Pallas kernels, call(): pl.pallas_call(kernel, out_shape=[jax.ShapeDtypeStruct(shape, dtype) for...  33.9 us
    ppermute x9, waiting for transfers between devices, permute(): return lax.ppermute(block, 'orb', pairs)  21.3 us
  transfers between devices with their start and end apart: 9, of which 2 were waited for; matrix products, arithmetic and copies ran while one was open for 2% of the time, Pallas kernels for 20%

profile of v4, /device:TPU:7, one launch (start us, length us, event | category | flops | bytes accessed | tf_op | source)
XLA Modules:
  0.0 155.5 jit_solution(5299176729551490295)
XLA Ops:
  0.0 0.7 collective-permute-start.1
  1.3 1.2 shard_map.65
  2.6 0.0 copy-start
  2.6 0.0 copy-start.1
  2.6 0.9 collective-permute-start.2
  3.5 1.4 shard_map.67
  4.9 0.8 collective-permute-start.4
  5.7 3.1 %collective-permute-start.3 = (f32[640,1024]{1,0:T(8,128)}, f32[640,1024]{1,0:T(8,128)S(1)}, u32[]{:S(2)}, u32[]{:S(2)}) collective-permute-start(f32[640,1024]{1,0:T(8,128)} %bitcast.own.source), channel_id=1, source_target_pairs={{1,2},{3,4},{5,6},{9,10},{11,12},{13,14},{2,1},{4,3},{6,5},{10,9},... | collective-permute-start | bytes 7864328 | tf_op jit(solution)/shard_map/ppermute | solution.py:15
  8.7 28.9 %collective-permute-start = (f32[1]{0:T(128)}, f32[1]{0:T(128)}, u32[]{:S(2)}, u32[]{:S(2)}) collective-permute-start(f32[1]{0:T(128)} %convert_element_type.3.rest_0_), channel_id=1, source_target_pairs={{0,1},{1,2},{2,3},{3,4},{4,5},{5,6},{6,7},{8,9},{9,10},{10,11},{11... | collective-permute-start | bytes 20 | tf_op jit(solution)/shard_map/ppermute | solution.py:15
  37.7 0.1 broadcast_in_dim.12.vcol.refs_8_.refs_6_
  37.9 7.9 %shard_map.64 = (f32[640,1024]{1,0:T(8,128)S(1)}, bf16[640,3072]{1,0:T(8,128)(2,1)S(1)}) custom-call(s32[16]{0:T(128)S(1)} %copy-done, f32[16]{0:T(128)S(1)} %copy-done.1, f32[640,1024]{1,0:T(8,128)} %bitcast.own.source, f32[1,640]{1,0:T(1,128)S(1)} %broadcast_in_dim.9.vrow.refs_7_.refs_5_, f32[640,1]{1,0:T(8,128)S(1)} %broadcast_in_dim.12.vcol.refs_8_.refs_6_), custom_call_target="tpu_custom_call" | custom-call | flops 5033164800 | bytes 8000000 | tf_op jit(solution)/shard_map/pallas_call | solution.py:220
  45.8 7.3 %shard_map.66 = (f32[640,1024]{1,0:T(8,128)S(1)}, f32[8,128]{1,0:T(8,128)S(1)}) custom-call(s32[16]{0:T(128)S(1)} %copy-done, f32[16]{0:T(128)S(1)} %copy-done.1, s32[1]{0:T(128)S(6)} %copy.12.refs_2_, f32[1]{0:T(128)} %collective-permute-done.refs_3_, s32[8]{0:T(128)S(1)} %copy-done.2, bf16[640,3072]{1,0:T(8,128)(2,1)S(1)} %get-tuple-element.18.refs_5_.refs_1_.own, ...), custom_call_target="tpu_custom_call" | custom-call | flops 5033164800 | bytes 8000000 | tf_op jit(solution)/shard_map/pallas_call | solution.py:220
  53.2 1.7 %slice.7 = f32[512,1024]{1,0:T(8,128)S(1)} slice(f32[640,1024]{1,0:T(8,128)} %bitcast.own.source), slice={[0:512], [0:1024]} | slice | bytes 4194304 | tf_op jit(solution)/shard_map/slice | solution.py:293
  54.9 58.6 %collective-permute-start.8 = (f32[512,1024]{1,0:T(8,128)S(1)}, f32[512,1024]{1,0:T(8,128)S(1)}, u32[]{:S(2)}, u32[]{:S(2)}) collective-permute-start(f32[512,1024]{1,0:T(8,128)S(1)} %slice.7), channel_id=1, source_target_pairs={{1,9},{2,10},{3,11},{4,12},{5,13},{6,14},{9,1},{10,2},{11,3},{12,4... | collective-permute-start | bytes 6291464 | tf_op jit(solution)/shard_map/ppermute | solution.py:15
  113.5 0.8 collective-permute-start.7
  114.2 0.7 collective-permute-start.5
  115.0 1.1 slice.6
  116.1 1.9 %collective-permute-start.6 = (f32[128,1024]{1,0:T(8,128)S(1)}, f32[128,1024]{1,0:T(8,128)S(1)}, u32[]{:S(2)}, u32[]{:S(2)}) collective-permute-start(f32[128,1024]{1,0:T(8,128)S(1)} %slice.6), channel_id=1, source_target_pairs={{1,9},{2,10},{3,11},{4,12},{5,13},{6,14},{9,1},{10,2},{11,3},{12,4... | collective-permute-start | bytes 1572872 | tf_op jit(solution)/shard_map/ppermute | solution.py:15
  118.0 6.4 %shard_map.68.acc = f32[640,1024]{1,0:T(8,128)S(1)} custom-call(f32[8,128]{1,0:T(8,128)S(1)} %get-tuple-element.21.refs_0_.later, bf16[640,3072]{1,0:T(8,128)(2,1)S(1)} %get-tuple-element.18.refs_5_.refs_1_.own, f32[640,1024]{1,0:T(8,128)S(1)} %collective-permute-done.3.refs_2_, f32[384,1024]{1,0:T(8,128)S(1)} %collective-permute-done.4.refs_3_, ...), custom_call_target="tpu_custom_call" | custom-call | flops 5033164800 | bytes 8000000 | tf_op jit(solution)/shard_map/pallas_call | solution.py:220
  124.5 2.5 %shard_map.69.own_turned = bf16[3072,640]{1,0:T(8,128)(2,1)S(1)} custom-call(f32[640,1024]{1,0:T(8,128)} %bitcast.own.source), custom_call_target="tpu_custom_call" | custom-call | bytes 8000000 | tf_op jit(solution)/shard_map/pallas_call | solution.py:220
  127.0 19.9 %collective-permute-done.8.rest = f32[512,1024]{1,0:T(8,128)S(1)} collective-permute-done((f32[512,1024]{1,0:T(8,128)S(1)}, f32[512,1024]{1,0:T(8,128)S(1)}, u32[]{:S(2)}, u32[]{:S(2)}) %collective-permute-start.8) | collective-permute-done | bytes 2097184 | tf_op jit(solution)/shard_map/ppermute | solution.py:15
  146.8 4.2 %shard_map.70 = (f32[640,1024]{1,0:T(8,128)S(1)}, f32[640,512]{1,0:T(8,128)S(1)}, bf16[1536,1024]{1,0:T(8,128)(2,1)S(1)}) custom-call(f32[8,128]{1,0:T(8,128)S(1)} %get-tuple-element.21.refs_0_.later, bf16[640,3072]{1,0:T(8,128)(2,1)S(1)} %get-tuple-element.18.refs_5_.refs_1_.own, f32[384,1024]{1,0:T(8,128)S(1)} %collective-permute-done.7.late0, ...), custom_call_target="tpu_custom_call" | custom-call | flops 2516582400 | bytes 8000000 | tf_op jit(solution)/shard_map/pallas_call | solution.py:220
  151.0 1.4 collective-permute-done.6.rest
  152.4 2.9 %shard_map.71 = f32[640,1024]{1,0:T(8,128)} custom-call(f32[8,128]{1,0:T(8,128)S(1)} %get-tuple-element.21.refs_0_.later, bf16[3072,640]{1,0:T(8,128)(2,1)S(1)} %shard_map.69.own_turned, f32[264,1024]{1,0:T(8,128)S(1)} %collective-permute-done.5.late1.late, f32[128,1024]{1,0:T(8,128)S(1)} %collective-permute-done.6.rest, ...), custom_call_target="tpu_custom_call" | custom-call | flops 2516582400 | bytes 8000000 | tf_op jit(solution)/shard_map/pallas_call | solution.py:220
  (14 shorter events, 0.0 us)
Async XLA Ops:
  0.0 45.8 %collective-permute-start.1 = (f32[640,1024]{1,0:T(8,128)}, f32[640,1024]{1,0:T(8,128)S(1)}, u32[]{:S(2)}, u32[]{:S(2)}) collective-permute-start(f32[640,1024]{1,0:T(8,128)} %bitcast.own.source), channel_id=1, source_target_pairs={{0,1},{1,0},{2,3},{3,2},{4,5},{5,4},{6,7},{7,6},{8,9},{9,8},{10,11... | collective-permute-start | bytes 7864328 | tf_op jit(solution)/shard_map/ppermute | solution.py:15
  2.6 35.1 %copy-start.3 = (f32[640]{0:T(1024)S(1)}, f32[640]{0:T(1024)}, u32[]{:S(2)}) copy-start(f32[640]{0:T(1024)} %param.8) | copy-start | bytes 7684
  2.6 35.3 %copy-start = (s32[16]{0:T(128)S(1)}, s32[16]{0:T(128)}, u32[]{:S(2)}) copy-start(s32[16]{0:T(128)} %refs_0_.1) | copy-start | bytes 196
  2.6 35.3 %copy-start.1 = (f32[16]{0:T(128)S(1)}, f32[16]{0:T(128)}, u32[]{:S(2)}) copy-start(f32[16]{0:T(128)} %refs_1_.1) | copy-start | bytes 196
  2.6 43.2 %collective-permute-start.2 = (f32[264,1024]{1,0:T(8,128)S(1)}, f32[264,1024]{1,0:T(8,128)S(1)}, u32[]{:S(2)}, u32[]{:S(2)}) collective-permute-start(f32[264,1024]{1,0:T(8,128)S(1)} %shard_map.65), channel_id=1, source_target_pairs={{0,8},{7,15},{8,0},{15,7},{16,24},{23,31},{24,16},{31,23}} | collective-permute-start | bytes 3244040 | tf_op jit(solution)/shard_map/ppermute | solution.py:15
  4.9 108.6 %collective-permute-start.4 = (f32[384,1024]{1,0:T(8,128)S(1)}, f32[384,1024]{1,0:T(8,128)S(1)}, u32[]{:S(2)}, u32[]{:S(2)}) collective-permute-start(f32[384,1024]{1,0:T(8,128)S(1)} %shard_map.67), channel_id=1, source_target_pairs={{0,8},{7,15},{8,0},{15,7},{16,24},{23,31},{24,16},{31,23}} | collective-permute-start | bytes 4718600 | tf_op jit(solution)/shard_map/ppermute | solution.py:15
  5.7 112.3 %collective-permute-start.3 = (f32[640,1024]{1,0:T(8,128)}, f32[640,1024]{1,0:T(8,128)S(1)}, u32[]{:S(2)}, u32[]{:S(2)}) collective-permute-start(f32[640,1024]{1,0:T(8,128)} %bitcast.own.source), channel_id=1, source_target_pairs={{1,2},{3,4},{5,6},{9,10},{11,12},{13,14},{2,1},{4,3},{6,5},{10,9},... | collective-permute-start | bytes 7864328 | tf_op jit(solution)/shard_map/ppermute | solution.py:15
  8.7 37.1 %collective-permute-start = (f32[1]{0:T(128)}, f32[1]{0:T(128)}, u32[]{:S(2)}, u32[]{:S(2)}) collective-permute-start(f32[1]{0:T(128)} %convert_element_type.3.rest_0_), channel_id=1, source_target_pairs={{0,1},{1,2},{2,3},{3,4},{4,5},{5,6},{6,7},{8,9},{9,10},{10,11},{11... | collective-permute-start | bytes 20 | tf_op jit(solution)/shard_map/ppermute | solution.py:15
  37.9 8.0 %copy-start.2 = (s32[8]{0:T(128)S(1)}, s32[8]{0:T(128)}, u32[]{:S(2)}) copy-start(s32[8]{0:T(128)} %refs_4_.1) | copy-start | bytes 100
  54.9 91.9 %collective-permute-start.8 = (f32[512,1024]{1,0:T(8,128)S(1)}, f32[512,1024]{1,0:T(8,128)S(1)}, u32[]{:S(2)}, u32[]{:S(2)}) collective-permute-start(f32[512,1024]{1,0:T(8,128)S(1)} %slice.7), channel_id=1, source_target_pairs={{1,9},{2,10},{3,11},{4,12},{5,13},{6,14},{9,1},{10,2},{11,3},{12,4... | collective-permute-start | bytes 6291464 | tf_op jit(solution)/shard_map/ppermute | solution.py:15
  113.5 13.5 %collective-permute-start.7 = (f32[384,1024]{1,0:T(8,128)S(1)}, f32[384,1024]{1,0:T(8,128)S(1)}, u32[]{:S(2)}, u32[]{:S(2)}) collective-permute-start(f32[384,1024]{1,0:T(8,128)S(1)} %collective-permute-done.4.refs_3_), channel_id=1, source_target_pairs={{0,7},{8,15},{7,0},{15,8},{16,23},{24,31},{23,16},{31,24}} | collective-permute-start | bytes 4718600 | tf_op jit(solution)/shard_map/ppermute | solution.py:15
  114.2 12.7 %collective-permute-start.5 = (f32[264,1024]{1,0:T(8,128)S(1)}, f32[264,1024]{1,0:T(8,128)S(1)}, u32[]{:S(2)}, u32[]{:S(2)}) collective-permute-start(f32[264,1024]{1,0:T(8,128)S(1)} %collective-permute-done.2.refs_4_), channel_id=1, source_target_pairs={{0,7},{8,15},{7,0},{15,8},{16,23},{24,31},{23,16},{31,24}} | collective-permute-start | bytes 3244040 | tf_op jit(solution)/shard_map/ppermute | solution.py:15
  116.1 36.4 %collective-permute-start.6 = (f32[128,1024]{1,0:T(8,128)S(1)}, f32[128,1024]{1,0:T(8,128)S(1)}, u32[]{:S(2)}, u32[]{:S(2)}) collective-permute-start(f32[128,1024]{1,0:T(8,128)S(1)} %slice.6), channel_id=1, source_target_pairs={{1,9},{2,10},{3,11},{4,12},{5,13},{6,14},{9,1},{10,2},{11,3},{12,4... | collective-permute-start | bytes 1572872 | tf_op jit(solution)/shard_map/ppermute | solution.py:15

commit v5 on v4

--- a/solution.py
+++ b/solution.py
@@ -200,12 +200,22 @@
     copies = []
     for i, columns in enumerate(column_blocks(acc.shape[1])):
         result[0:cut, columns] = acc[0:cut, columns] + dot(wide_ab[...], tall[:, columns], NN)
+        copies.append(
+            pltpu.make_async_copy(
+                result.at[0:cut, columns], out.at[0:cut, columns], out_sems.at[2 * i]
+            )
+        )
+        copies[-1].start()
         result[cut:, columns] = (
             acc[cut:, columns]
             + dot(wide_ba[...], tall_a[:, columns], NN)
             + dot(wide_bb[...], tall[:, columns], NN)
         )
-        copies.append(pltpu.make_async_copy(result.at[:, columns], out.at[:, columns], out_sems.at[i]))
+        copies.append(
+            pltpu.make_async_copy(
+                result.at[cut:, columns], out.at[cut:, columns], out_sems.at[2 * i + 1]
+            )
+        )
         copies[-1].start()
     for copy in copies:
         copy.wait()
@@ -319,7 +329,7 @@
             pltpu.VMEM((size, 3 * cut), bf16),
             pltpu.VMEM((size, 3 * size), bf16),
             pltpu.VMEM((rows, k), f32),
-            pltpu.SemaphoreType.DMA((4,)),
+            pltpu.SemaphoreType.DMA((8,)),
         ],
         flops // 2,
         26_000_000,

time: 156 us -> 156 us (level)
  no operation moved by 1% of the time
where the time goes in v5:
time: 156 us
  starting transfers between devices  96.3 us (62%)
  Pallas kernels  33.9 us (22%)
  waiting for transfers between devices  21.3 us (14%)
  local copies, waits for them, and re-layouts  2.98 us (2%)
    ppermute x9, starting transfers between devices, permute(): return lax.ppermute(block, 'orb', pairs)  96.3 us
    pallas_call x8, Pallas kernels, call(): pl.pallas_call(kernel, out_shape=[jax.ShapeDtypeStruct(shape, dtype) for...  33.9 us
    ppermute x9, waiting for transfers between devices, permute(): return lax.ppermute(block, 'orb', pairs)  21.3 us
  transfers between devices with their start and end apart: 9, of which 2 were waited for; matrix products, arithmetic and copies ran while one was open for 2% of the time, Pallas kernels for 20%

profile of v5, /device:TPU:7, one launch (start us, length us, event | category | flops | bytes accessed | tf_op | source)
XLA Modules:
  0.0 155.5 jit_solution(8755930497469258427)
XLA Ops:
  0.0 0.7 collective-permute-start.1
  1.3 1.2 shard_map.65
  2.6 0.0 copy-start
  2.6 0.0 copy-start.1
  2.6 0.9 collective-permute-start.2
  3.5 1.4 shard_map.67
  4.9 0.8 collective-permute-start.4
  5.7 3.1 %collective-permute-start.3 = (f32[640,1024]{1,0:T(8,128)}, f32[640,1024]{1,0:T(8,128)S(1)}, u32[]{:S(2)}, u32[]{:S(2)}) collective-permute-start(f32[640,1024]{1,0:T(8,128)} %bitcast.own.source), channel_id=1, source_target_pairs={{1,2},{3,4},{5,6},{9,10},{11,12},{13,14},{2,1},{4,3},{6,5},{10,9},... | collective-permute-start | bytes 7864328 | tf_op jit(solution)/shard_map/ppermute | solution.py:15
  8.7 28.9 %collective-permute-start = (f32[1]{0:T(128)}, f32[1]{0:T(128)}, u32[]{:S(2)}, u32[]{:S(2)}) collective-permute-start(f32[1]{0:T(128)} %convert_element_type.3.rest_0_), channel_id=1, source_target_pairs={{0,1},{1,2},{2,3},{3,4},{4,5},{5,6},{6,7},{8,9},{9,10},{10,11},{11... | collective-permute-start | bytes 20 | tf_op jit(solution)/shard_map/ppermute | solution.py:15
  37.7 0.1 broadcast_in_dim.12.vcol.refs_8_.refs_6_
  37.9 7.9 %shard_map.64 = (f32[640,1024]{1,0:T(8,128)S(1)}, bf16[640,3072]{1,0:T(8,128)(2,1)S(1)}) custom-call(s32[16]{0:T(128)S(1)} %copy-done, f32[16]{0:T(128)S(1)} %copy-done.1, f32[640,1024]{1,0:T(8,128)} %bitcast.own.source, f32[1,640]{1,0:T(1,128)S(1)} %broadcast_in_dim.9.vrow.refs_7_.refs_5_, f32[640,1]{1,0:T(8,128)S(1)} %broadcast_in_dim.12.vcol.refs_8_.refs_6_), custom_call_target="tpu_custom_call" | custom-call | flops 5033164800 | bytes 8000000 | tf_op jit(solution)/shard_map/pallas_call | solution.py:230
  45.8 7.3 %shard_map.66 = (f32[640,1024]{1,0:T(8,128)S(1)}, f32[8,128]{1,0:T(8,128)S(1)}) custom-call(s32[16]{0:T(128)S(1)} %copy-done, f32[16]{0:T(128)S(1)} %copy-done.1, s32[1]{0:T(128)S(6)} %copy.12.refs_2_, f32[1]{0:T(128)} %collective-permute-done.refs_3_, s32[8]{0:T(128)S(1)} %copy-done.2, bf16[640,3072]{1,0:T(8,128)(2,1)S(1)} %get-tuple-element.18.refs_5_.refs_1_.own, ...), custom_call_target="tpu_custom_call" | custom-call | flops 5033164800 | bytes 8000000 | tf_op jit(solution)/shard_map/pallas_call | solution.py:230
  53.2 1.7 %slice.7 = f32[512,1024]{1,0:T(8,128)S(1)} slice(f32[640,1024]{1,0:T(8,128)} %bitcast.own.source), slice={[0:512], [0:1024]} | slice | bytes 4194304 | tf_op jit(solution)/shard_map/slice | solution.py:303
  54.9 58.6 %collective-permute-start.8 = (f32[512,1024]{1,0:T(8,128)S(1)}, f32[512,1024]{1,0:T(8,128)S(1)}, u32[]{:S(2)}, u32[]{:S(2)}) collective-permute-start(f32[512,1024]{1,0:T(8,128)S(1)} %slice.7), channel_id=1, source_target_pairs={{1,9},{2,10},{3,11},{4,12},{5,13},{6,14},{9,1},{10,2},{11,3},{12,4... | collective-permute-start | bytes 6291464 | tf_op jit(solution)/shard_map/ppermute | solution.py:15
  113.5 0.8 collective-permute-start.7
  114.2 0.7 collective-permute-start.5
  115.0 1.1 slice.6
  116.1 1.9 %collective-permute-start.6 = (f32[128,1024]{1,0:T(8,128)S(1)}, f32[128,1024]{1,0:T(8,128)S(1)}, u32[]{:S(2)}, u32[]{:S(2)}) collective-permute-start(f32[128,1024]{1,0:T(8,128)S(1)} %slice.6), channel_id=1, source_target_pairs={{1,9},{2,10},{3,11},{4,12},{5,13},{6,14},{9,1},{10,2},{11,3},{12,4... | collective-permute-start | bytes 1572872 | tf_op jit(solution)/shard_map/ppermute | solution.py:15
  118.0 6.4 %shard_map.68.acc = f32[640,1024]{1,0:T(8,128)S(1)} custom-call(f32[8,128]{1,0:T(8,128)S(1)} %get-tuple-element.21.refs_0_.later, bf16[640,3072]{1,0:T(8,128)(2,1)S(1)} %get-tuple-element.18.refs_5_.refs_1_.own, f32[640,1024]{1,0:T(8,128)S(1)} %collective-permute-done.3.refs_2_, f32[384,1024]{1,0:T(8,128)S(1)} %collective-permute-done.4.refs_3_, ...), custom_call_target="tpu_custom_call" | custom-call | flops 5033164800 | bytes 8000000 | tf_op jit(solution)/shard_map/pallas_call | solution.py:230
  124.5 2.5 %shard_map.69.own_turned = bf16[3072,640]{1,0:T(8,128)(2,1)S(1)} custom-call(f32[640,1024]{1,0:T(8,128)} %bitcast.own.source), custom_call_target="tpu_custom_call" | custom-call | bytes 8000000 | tf_op jit(solution)/shard_map/pallas_call | solution.py:230
  127.0 19.9 %collective-permute-done.8.rest = f32[512,1024]{1,0:T(8,128)S(1)} collective-permute-done((f32[512,1024]{1,0:T(8,128)S(1)}, f32[512,1024]{1,0:T(8,128)S(1)}, u32[]{:S(2)}, u32[]{:S(2)}) %collective-permute-start.8) | collective-permute-done | bytes 2097184 | tf_op jit(solution)/shard_map/ppermute | solution.py:15
  146.8 4.2 %shard_map.70 = (f32[640,1024]{1,0:T(8,128)S(1)}, f32[640,512]{1,0:T(8,128)S(1)}, bf16[1536,1024]{1,0:T(8,128)(2,1)S(1)}) custom-call(f32[8,128]{1,0:T(8,128)S(1)} %get-tuple-element.21.refs_0_.later, bf16[640,3072]{1,0:T(8,128)(2,1)S(1)} %get-tuple-element.18.refs_5_.refs_1_.own, f32[384,1024]{1,0:T(8,128)S(1)} %collective-permute-done.7.late0, ...), custom_call_target="tpu_custom_call" | custom-call | flops 2516582400 | bytes 8000000 | tf_op jit(solution)/shard_map/pallas_call | solution.py:230
  151.0 1.4 collective-permute-done.6.rest
  152.4 2.9 %shard_map.71 = f32[640,1024]{1,0:T(8,128)} custom-call(f32[8,128]{1,0:T(8,128)S(1)} %get-tuple-element.21.refs_0_.later, bf16[3072,640]{1,0:T(8,128)(2,1)S(1)} %shard_map.69.own_turned, f32[264,1024]{1,0:T(8,128)S(1)} %collective-permute-done.5.late1.late, f32[128,1024]{1,0:T(8,128)S(1)} %collective-permute-done.6.rest, ...), custom_call_target="tpu_custom_call" | custom-call | flops 2516582400 | bytes 8000000 | tf_op jit(solution)/shard_map/pallas_call | solution.py:230
  (14 shorter events, 0.0 us)
Async XLA Ops:
  0.0 45.8 %collective-permute-start.1 = (f32[640,1024]{1,0:T(8,128)}, f32[640,1024]{1,0:T(8,128)S(1)}, u32[]{:S(2)}, u32[]{:S(2)}) collective-permute-start(f32[640,1024]{1,0:T(8,128)} %bitcast.own.source), channel_id=1, source_target_pairs={{0,1},{1,0},{2,3},{3,2},{4,5},{5,4},{6,7},{7,6},{8,9},{9,8},{10,11... | collective-permute-start | bytes 7864328 | tf_op jit(solution)/shard_map/ppermute | solution.py:15
  2.6 35.1 %copy-start.3 = (f32[640]{0:T(1024)S(1)}, f32[640]{0:T(1024)}, u32[]{:S(2)}) copy-start(f32[640]{0:T(1024)} %param.8) | copy-start | bytes 7684
  2.6 35.3 %copy-start = (s32[16]{0:T(128)S(1)}, s32[16]{0:T(128)}, u32[]{:S(2)}) copy-start(s32[16]{0:T(128)} %refs_0_.1) | copy-start | bytes 196
  2.6 35.3 %copy-start.1 = (f32[16]{0:T(128)S(1)}, f32[16]{0:T(128)}, u32[]{:S(2)}) copy-start(f32[16]{0:T(128)} %refs_1_.1) | copy-start | bytes 196
  2.6 43.2 %collective-permute-start.2 = (f32[264,1024]{1,0:T(8,128)S(1)}, f32[264,1024]{1,0:T(8,128)S(1)}, u32[]{:S(2)}, u32[]{:S(2)}) collective-permute-start(f32[264,1024]{1,0:T(8,128)S(1)} %shard_map.65), channel_id=1, source_target_pairs={{0,8},{7,15},{8,0},{15,7},{16,24},{23,31},{24,16},{31,23}} | collective-permute-start | bytes 3244040 | tf_op jit(solution)/shard_map/ppermute | solution.py:15
  4.9 108.6 %collective-permute-start.4 = (f32[384,1024]{1,0:T(8,128)S(1)}, f32[384,1024]{1,0:T(8,128)S(1)}, u32[]{:S(2)}, u32[]{:S(2)}) collective-permute-start(f32[384,1024]{1,0:T(8,128)S(1)} %shard_map.67), channel_id=1, source_target_pairs={{0,8},{7,15},{8,0},{15,7},{16,24},{23,31},{24,16},{31,23}} | collective-permute-start | bytes 4718600 | tf_op jit(solution)/shard_map/ppermute | solution.py:15
  5.7 112.3 %collective-permute-start.3 = (f32[640,1024]{1,0:T(8,128)}, f32[640,1024]{1,0:T(8,128)S(1)}, u32[]{:S(2)}, u32[]{:S(2)}) collective-permute-start(f32[640,1024]{1,0:T(8,128)} %bitcast.own.source), channel_id=1, source_target_pairs={{1,2},{3,4},{5,6},{9,10},{11,12},{13,14},{2,1},{4,3},{6,5},{10,9},... | collective-permute-start | bytes 7864328 | tf_op jit(solution)/shard_map/ppermute | solution.py:15
  8.7 37.1 %collective-permute-start = (f32[1]{0:T(128)}, f32[1]{0:T(128)}, u32[]{:S(2)}, u32[]{:S(2)}) collective-permute-start(f32[1]{0:T(128)} %convert_element_type.3.rest_0_), channel_id=1, source_target_pairs={{0,1},{1,2},{2,3},{3,4},{4,5},{5,6},{6,7},{8,9},{9,10},{10,11},{11... | collective-permute-start | bytes 20 | tf_op jit(solution)/shard_map/ppermute | solution.py:15
  37.9 8.0 %copy-start.2 = (s32[8]{0:T(128)S(1)}, s32[8]{0:T(128)}, u32[]{:S(2)}) copy-start(s32[8]{0:T(128)} %refs_4_.1) | copy-start | bytes 100
  54.9 91.9 %collective-permute-start.8 = (f32[512,1024]{1,0:T(8,128)S(1)}, f32[512,1024]{1,0:T(8,128)S(1)}, u32[]{:S(2)}, u32[]{:S(2)}) collective-permute-start(f32[512,1024]{1,0:T(8,128)S(1)} %slice.7), channel_id=1, source_target_pairs={{1,9},{2,10},{3,11},{4,12},{5,13},{6,14},{9,1},{10,2},{11,3},{12,4... | collective-permute-start | bytes 6291464 | tf_op jit(solution)/shard_map/ppermute | solution.py:15
  113.5 13.5 %collective-permute-start.7 = (f32[384,1024]{1,0:T(8,128)S(1)}, f32[384,1024]{1,0:T(8,128)S(1)}, u32[]{:S(2)}, u32[]{:S(2)}) collective-permute-start(f32[384,1024]{1,0:T(8,128)S(1)} %collective-permute-done.4.refs_3_), channel_id=1, source_target_pairs={{0,7},{8,15},{7,0},{15,8},{16,23},{24,31},{23,16},{31,24}} | collective-permute-start | bytes 4718600 | tf_op jit(solution)/shard_map/ppermute | solution.py:15
  114.2 12.7 %collective-permute-start.5 = (f32[264,1024]{1,0:T(8,128)S(1)}, f32[264,1024]{1,0:T(8,128)S(1)}, u32[]{:S(2)}, u32[]{:S(2)}) collective-permute-start(f32[264,1024]{1,0:T(8,128)S(1)} %collective-permute-done.2.refs_4_), channel_id=1, source_target_pairs={{0,7},{8,15},{7,0},{15,8},{16,23},{24,31},{23,16},{31,24}} | collective-permute-start | bytes 3244040 | tf_op jit(solution)/shard_map/ppermute | solution.py:15
  116.1 36.4 %collective-permute-start.6 = (f32[128,1024]{1,0:T(8,128)S(1)}, f32[128,1024]{1,0:T(8,128)S(1)}, u32[]{:S(2)}, u32[]{:S(2)}) collective-permute-start(f32[128,1024]{1,0:T(8,128)S(1)} %slice.6), channel_id=1, source_target_pairs={{1,9},{2,10},{3,11},{4,12},{5,13},{6,14},{9,1},{10,2},{11,3},{12,4... | collective-permute-start | bytes 1572872 | tf_op jit(solution)/shard_map/ppermute | solution.py:15

commit v6 on v4

--- a/solution.py
+++ b/solution.py
@@ -282,15 +282,15 @@
         kernel_d, [small[0], small[1], (VMEM, own), *v],
         [((rows, k), f32), ((rows, 3 * k), bf16)], [right, wide, tall], flops, 32_000_000,
     )
-    (first,), acc = after((straight_slices[1],), acc)
+    (first, whole), acc = after((straight_slices[1], own), acc)
+    pieces, acc = after((whole[:cut], whole[cut:]), acc)
     late1 = permute(first, forwards)
     acc, later = call(
         lambda *refs: kernel_ab("A", *refs),
         [*small, (VMEM, own_three), (VMEM, mate), *v, (VMEM, acc)],
         [((rows, k), f32), ((8, 128), f32)], [right, wide, tall], flops, 32_000_000,
     )
-    (whole,), acc = after((own,), acc)
-    pieces = (whole[:cut], whole[cut:])
+    pieces, acc = after(pieces, acc)
     rest = [permute(piece, opposites) for piece in pieces]
     late = [permute(straight_slices[0], forwards), late1]
     (acc,) = call(

time: 156 us -> 154 us (0.987)
  the two profiles are of different devices: /device:TPU:7 before, /device:TPU:3 now
where the time goes in v6:
time: 154 us
  starting transfers between devices  96.3 us (63%)
  Pallas kernels  33.9 us (22%)
  waiting for transfers between devices  19.6 us (13%)
  local copies, waits for them, and re-layouts  2.98 us (2%)
    ppermute x9, starting transfers between devices, permute(): return lax.ppermute(block, 'orb', pairs)  96.3 us
    pallas_call x8, Pallas kernels, call(): pl.pallas_call(kernel, out_shape=[jax.ShapeDtypeStruct(shape, dtype) for...  33.9 us
    ppermute x9, waiting for transfers between devices, permute(): return lax.ppermute(block, 'orb', pairs)  19.6 us
  transfers between devices with their start and end apart: 9, of which 2 were waited for; matrix products, arithmetic and copies ran while one was open for 2% of the time, Pallas kernels for 20%

profile of v6, /device:TPU:3, one launch (start us, length us, event | category | flops | bytes accessed | tf_op | source)
XLA Modules:
  0.0 153.8 jit_solution(4589580393305458619)
XLA Ops:
  0.0 0.7 collective-permute-start.1
  1.3 1.2 shard_map.65
  2.6 0.0 copy-start
  2.6 0.0 copy-start.1
  2.6 0.9 collective-permute-start.2
  3.5 1.4 shard_map.67
  4.9 0.8 collective-permute-start.4
  5.7 3.1 %collective-permute-start.3 = (f32[640,1024]{1,0:T(8,128)}, f32[640,1024]{1,0:T(8,128)S(1)}, u32[]{:S(2)}, u32[]{:S(2)}) collective-permute-start(f32[640,1024]{1,0:T(8,128)} %bitcast.own.source), channel_id=1, source_target_pairs={{1,2},{3,4},{5,6},{9,10},{11,12},{13,14},{2,1},{4,3},{6,5},{10,9},... | collective-permute-start | bytes 7864328 | tf_op jit(solution)/shard_map/ppermute | solution.py:15
  8.7 28.9 %collective-permute-start = (f32[1]{0:T(128)}, f32[1]{0:T(128)}, u32[]{:S(2)}, u32[]{:S(2)}) collective-permute-start(f32[1]{0:T(128)} %convert_element_type.3.rest_0_), channel_id=1, source_target_pairs={{0,1},{1,2},{2,3},{3,4},{4,5},{5,6},{6,7},{8,9},{9,10},{10,11},{11... | collective-permute-start | bytes 20 | tf_op jit(solution)/shard_map/ppermute | solution.py:15
  37.7 0.1 broadcast_in_dim.12.vcol.refs_8_.refs_6_
  37.9 7.9 %shard_map.64 = (f32[640,1024]{1,0:T(8,128)S(1)}, bf16[640,3072]{1,0:T(8,128)(2,1)S(1)}) custom-call(s32[16]{0:T(128)S(1)} %copy-done, f32[16]{0:T(128)S(1)} %copy-done.1, f32[640,1024]{1,0:T(8,128)} %bitcast.own.source, f32[1,640]{1,0:T(1,128)S(1)} %broadcast_in_dim.9.vrow.refs_7_.refs_5_, f32[640,1]{1,0:T(8,128)S(1)} %broadcast_in_dim.12.vcol.refs_8_.refs_6_), custom_call_target="tpu_custom_call" | custom-call | flops 5033164800 | bytes 8000000 | tf_op jit(solution)/shard_map/pallas_call | solution.py:220
  45.8 1.7 %slice.6 = f32[512,1024]{1,0:T(8,128)S(1)} slice(f32[640,1024]{1,0:T(8,128)} %bitcast.own.source), slice={[0:512], [0:1024]} | slice | bytes 4194304 | tf_op jit(solution)/shard_map/slice | solution.py:286
  47.5 1.1 slice.7
  48.6 7.3 %shard_map.66 = (f32[640,1024]{1,0:T(8,128)S(1)}, f32[8,128]{1,0:T(8,128)S(1)}) custom-call(s32[16]{0:T(128)S(1)} %copy-done, f32[16]{0:T(128)S(1)} %copy-done.1, s32[1]{0:T(128)S(6)} %copy.12.refs_2_, f32[1]{0:T(128)} %collective-permute-done.refs_3_, s32[8]{0:T(128)S(1)} %copy-done.2, bf16[640,3072]{1,0:T(8,128)(2,1)S(1)} %get-tuple-element.23.refs_5_.refs_1_.own, ...), custom_call_target="tpu_custom_call" | custom-call | flops 5033164800 | bytes 8000000 | tf_op jit(solution)/shard_map/pallas_call | solution.py:220
  56.0 58.6 %collective-permute-start.8 = (f32[512,1024]{1,0:T(8,128)S(1)}, f32[512,1024]{1,0:T(8,128)S(1)}, u32[]{:S(2)}, u32[]{:S(2)}) collective-permute-start(f32[512,1024]{1,0:T(8,128)S(1)} %slice.6), channel_id=1, source_target_pairs={{1,9},{2,10},{3,11},{4,12},{5,13},{6,14},{9,1},{10,2},{11,3},{12,4... | collective-permute-start | bytes 6291464 | tf_op jit(solution)/shard_map/ppermute | solution.py:15
  114.6 0.8 collective-permute-start.7
  115.3 0.7 collective-permute-start.5
  116.1 1.9 %collective-permute-start.6 = (f32[128,1024]{1,0:T(8,128)S(1)}, f32[128,1024]{1,0:T(8,128)S(1)}, u32[]{:S(2)}, u32[]{:S(2)}) collective-permute-start(f32[128,1024]{1,0:T(8,128)S(1)} %slice.7), channel_id=1, source_target_pairs={{1,9},{2,10},{3,11},{4,12},{5,13},{6,14},{9,1},{10,2},{11,3},{12,4... | collective-permute-start | bytes 1572872 | tf_op jit(solution)/shard_map/ppermute | solution.py:15
  118.0 6.4 %shard_map.68.acc = f32[640,1024]{1,0:T(8,128)S(1)} custom-call(f32[8,128]{1,0:T(8,128)S(1)} %get-tuple-element.28.refs_0_.later, bf16[640,3072]{1,0:T(8,128)(2,1)S(1)} %get-tuple-element.23.refs_5_.refs_1_.own, f32[640,1024]{1,0:T(8,128)S(1)} %collective-permute-done.3.refs_2_, f32[384,1024]{1,0:T(8,128)S(1)} %collective-permute-done.4.refs_3_, ...), custom_call_target="tpu_custom_call" | custom-call | flops 5033164800 | bytes 8000000 | tf_op jit(solution)/shard_map/pallas_call | solution.py:220
  124.5 2.5 %shard_map.69.own_turned = bf16[3072,640]{1,0:T(8,128)(2,1)S(1)} custom-call(f32[640,1024]{1,0:T(8,128)} %bitcast.own.source), custom_call_target="tpu_custom_call" | custom-call | bytes 8000000 | tf_op jit(solution)/shard_map/pallas_call | solution.py:220
  127.0 18.1 %collective-permute-done.8.rest = f32[512,1024]{1,0:T(8,128)S(1)} collective-permute-done((f32[512,1024]{1,0:T(8,128)S(1)}, f32[512,1024]{1,0:T(8,128)S(1)}, u32[]{:S(2)}, u32[]{:S(2)}) %collective-permute-start.8) | collective-permute-done | bytes 2097184 | tf_op jit(solution)/shard_map/ppermute | solution.py:15
  145.1 4.2 %shard_map.70 = (f32[640,1024]{1,0:T(8,128)S(1)}, f32[640,512]{1,0:T(8,128)S(1)}, bf16[1536,1024]{1,0:T(8,128)(2,1)S(1)}) custom-call(f32[8,128]{1,0:T(8,128)S(1)} %get-tuple-element.28.refs_0_.later, bf16[640,3072]{1,0:T(8,128)(2,1)S(1)} %get-tuple-element.23.refs_5_.refs_1_.own, f32[384,1024]{1,0:T(8,128)S(1)} %collective-permute-done.7.late0, ...), custom_call_target="tpu_custom_call" | custom-call | flops 2516582400 | bytes 8000000 | tf_op jit(solution)/shard_map/pallas_call | solution.py:220
  149.3 1.4 collective-permute-done.6.rest
  150.7 2.9 %shard_map.71 = f32[640,1024]{1,0:T(8,128)} custom-call(f32[8,128]{1,0:T(8,128)S(1)} %get-tuple-element.28.refs_0_.later, bf16[3072,640]{1,0:T(8,128)(2,1)S(1)} %shard_map.69.own_turned, f32[264,1024]{1,0:T(8,128)S(1)} %collective-permute-done.5.late1.late, f32[128,1024]{1,0:T(8,128)S(1)} %collective-permute-done.6.rest, ...), custom_call_target="tpu_custom_call" | custom-call | flops 2516582400 | bytes 8000000 | tf_op jit(solution)/shard_map/pallas_call | solution.py:220
  (14 shorter events, 0.0 us)
Async XLA Ops:
  0.0 48.6 %collective-permute-start.1 = (f32[640,1024]{1,0:T(8,128)}, f32[640,1024]{1,0:T(8,128)S(1)}, u32[]{:S(2)}, u32[]{:S(2)}) collective-permute-start(f32[640,1024]{1,0:T(8,128)} %bitcast.own.source), channel_id=1, source_target_pairs={{0,1},{1,0},{2,3},{3,2},{4,5},{5,4},{6,7},{7,6},{8,9},{9,8},{10,11... | collective-permute-start | bytes 7864328 | tf_op jit(solution)/shard_map/ppermute | solution.py:15
  2.6 35.1 %copy-start.3 = (f32[640]{0:T(1024)S(1)}, f32[640]{0:T(1024)}, u32[]{:S(2)}) copy-start(f32[640]{0:T(1024)} %param.8) | copy-start | bytes 7684
  2.6 35.3 %copy-start = (s32[16]{0:T(128)S(1)}, s32[16]{0:T(128)}, u32[]{:S(2)}) copy-start(s32[16]{0:T(128)} %refs_0_.1) | copy-start | bytes 196
  2.6 35.3 %copy-start.1 = (f32[16]{0:T(128)S(1)}, f32[16]{0:T(128)}, u32[]{:S(2)}) copy-start(f32[16]{0:T(128)} %refs_1_.1) | copy-start | bytes 196
  2.6 43.2 %collective-permute-start.2 = (f32[264,1024]{1,0:T(8,128)S(1)}, f32[264,1024]{1,0:T(8,128)S(1)}, u32[]{:S(2)}, u32[]{:S(2)}) collective-permute-start(f32[264,1024]{1,0:T(8,128)S(1)} %shard_map.65), channel_id=1, source_target_pairs={{0,8},{7,15},{8,0},{15,7},{16,24},{23,31},{24,16},{31,23}} | collective-permute-start | bytes 3244040 | tf_op jit(solution)/shard_map/ppermute | solution.py:15
  4.9 109.7 %collective-permute-start.4 = (f32[384,1024]{1,0:T(8,128)S(1)}, f32[384,1024]{1,0:T(8,128)S(1)}, u32[]{:S(2)}, u32[]{:S(2)}) collective-permute-start(f32[384,1024]{1,0:T(8,128)S(1)} %shard_map.67), channel_id=1, source_target_pairs={{0,8},{7,15},{8,0},{15,7},{16,24},{23,31},{24,16},{31,23}} | collective-permute-start | bytes 4718600 | tf_op jit(solution)/shard_map/ppermute | solution.py:15
  5.7 112.3 %collective-permute-start.3 = (f32[640,1024]{1,0:T(8,128)}, f32[640,1024]{1,0:T(8,128)S(1)}, u32[]{:S(2)}, u32[]{:S(2)}) collective-permute-start(f32[640,1024]{1,0:T(8,128)} %bitcast.own.source), channel_id=1, source_target_pairs={{1,2},{3,4},{5,6},{9,10},{11,12},{13,14},{2,1},{4,3},{6,5},{10,9},... | collective-permute-start | bytes 7864328 | tf_op jit(solution)/shard_map/ppermute | solution.py:15
  8.7 39.9 %collective-permute-start = (f32[1]{0:T(128)}, f32[1]{0:T(128)}, u32[]{:S(2)}, u32[]{:S(2)}) collective-permute-start(f32[1]{0:T(128)} %convert_element_type.3.rest_0_), channel_id=1, source_target_pairs={{0,1},{1,2},{2,3},{3,4},{4,5},{5,6},{6,7},{8,9},{9,10},{10,11},{11... | collective-permute-start | bytes 20 | tf_op jit(solution)/shard_map/ppermute | solution.py:15
  45.8 2.9 %copy-start.2 = (s32[8]{0:T(128)S(1)}, s32[8]{0:T(128)}, u32[]{:S(2)}) copy-start(s32[8]{0:T(128)} %refs_4_.1) | copy-start | bytes 100
  56.0 89.1 %collective-permute-start.8 = (f32[512,1024]{1,0:T(8,128)S(1)}, f32[512,1024]{1,0:T(8,128)S(1)}, u32[]{:S(2)}, u32[]{:S(2)}) collective-permute-start(f32[512,1024]{1,0:T(8,128)S(1)} %slice.6), channel_id=1, source_target_pairs={{1,9},{2,10},{3,11},{4,12},{5,13},{6,14},{9,1},{10,2},{11,3},{12,4... | collective-permute-start | bytes 6291464 | tf_op jit(solution)/shard_map/ppermute | solution.py:15
  114.6 12.4 %collective-permute-start.7 = (f32[384,1024]{1,0:T(8,128)S(1)}, f32[384,1024]{1,0:T(8,128)S(1)}, u32[]{:S(2)}, u32[]{:S(2)}) collective-permute-start(f32[384,1024]{1,0:T(8,128)S(1)} %collective-permute-done.4.refs_3_), channel_id=1, source_target_pairs={{0,7},{8,15},{7,0},{15,8},{16,23},{24,31},{23,16},{31,24}} | collective-permute-start | bytes 4718600 | tf_op jit(solution)/shard_map/ppermute | solution.py:15
  115.3 11.6 %collective-permute-start.5 = (f32[264,1024]{1,0:T(8,128)S(1)}, f32[264,1024]{1,0:T(8,128)S(1)}, u32[]{:S(2)}, u32[]{:S(2)}) collective-permute-start(f32[264,1024]{1,0:T(8,128)S(1)} %collective-permute-done.2.refs_4_), channel_id=1, source_target_pairs={{0,7},{8,15},{7,0},{15,8},{16,23},{24,31},{23,16},{31,24}} | collective-permute-start | bytes 3244040 | tf_op jit(solution)/shard_map/ppermute | solution.py:15
  116.1 34.6 %collective-permute-start.6 = (f32[128,1024]{1,0:T(8,128)S(1)}, f32[128,1024]{1,0:T(8,128)S(1)}, u32[]{:S(2)}, u32[]{:S(2)}) collective-permute-start(f32[128,1024]{1,0:T(8,128)S(1)} %slice.7), channel_id=1, source_target_pairs={{1,9},{2,10},{3,11},{4,12},{5,13},{6,14},{9,1},{10,2},{11,3},{12,4... | collective-permute-start | bytes 1572872 | tf_op jit(solution)/shard_map/ppermute | solution.py:15
